TPU v7x, 32 devices: a whole 2x2x4 slice. The times are simulated.
32 devices in a mesh: groups: 2 (over x), cell: 16 (over z, y, core).
Axes of the slice: x: 2, y: 2, z: 4, core: 2. Of those that a mesh axis runs over, the one named last changes fastest.
Arguments:
- frames: bfloat16 [4096, 8, 512], P(('groups', 'cell')), parts along dimension 0
- norm_time: float32 [512], replicated, may hold values from 0.1 to 1.9
- t_wq: bfloat16 [512, 512], replicated
- t_wkv: bfloat16 [512, 1024], replicated
- t_wo: bfloat16 [512, 512], replicated, may hold values from -0.25 to 0.25
- norm_space: float32 [512], replicated, may hold values from 0.1 to 1.9
- s_wq: bfloat16 [512, 512], replicated
- s_wkv: bfloat16 [512, 1024], replicated
- s_wo: bfloat16 [512, 512], replicated, may hold values from -0.25 to 0.25
- norm_mlp: float32 [512], replicated, may hold values from 0.1 to 1.9
- w_gate: bfloat16 [512, 2048], replicated, may hold values from -0.25 to 0.25
- w_up: bfloat16 [512, 2048], replicated, may hold values from -0.25 to 0.25
- w_down: bfloat16 [2048, 512], replicated, may hold values from -0.125 to 0.125
- nbr_blocks: int32 [32, 3], P(('groups', 'cell')), parts along dimension 0, may hold values from 0 to 15, as said below
- nbr_count: int32 [32], P(('groups', 'cell')), parts along dimension 0, may hold values from 1 to 3, as said below
Outputs:
- forecast_rows: bfloat16 [4096, 8, 512], P(('groups', 'cell')), parts along dimension 0
There are 2 independent parts, one for each index of `groups`. A program takes and returns all parts, laid end to end along the dimension named above; an argument that names none is the same for every part. Nothing has to cross between parts.
Inputs may be any that keep to these rules, and one draw needn't show every extreme that they name: `nbr_blocks`: row b lists distinct blocks b + o modulo 16 with 1 <= |o| <= 2; only the first nbr_count[b] entries of a row are used, the others are such blocks too. Block 0 lists block 15 and block 1 lists block 0, each as its first entry. `nbr_count`: some block uses all 3 entries and some block uses one.
All inputs are finite; a program needn't handle non-finite values.
Results may differ from a plain program's by a relative error of at most 0.018.
Values may be sent and summed in bfloat16 or wider, within the bound.
No kernel may reach another device: no remote copies, remote signals or barrier semaphores. Data moves between devices by JAX's collectives and lax.ppermute only.
A program may use at most 128 MiB of HBM per device.

v0:
```python
import functools
import math

import jax
import jax.numpy as jnp
from jax import lax
from jax.experimental import pallas as pl
from jax.experimental.pallas import tpu as pltpu
from jax.sharding import PartitionSpec as P

HEAD_DIM = 64
EPS = 1e-05
NEG = -1e30
PIECES = 4
NOTE = 8
AHEAD_T = 8
AHEAD_S = 3
MIB = 1 << 20


f32 = jnp.float32
bf16 = jnp.bfloat16


def normed(wide, gain):
    scale = lax.rsqrt(jnp.mean(wide * wide, axis=-1, keepdims=True) + EPS)
    return (wide * scale * gain).astype(bf16)


def mm(a, b):
    return jnp.dot(a, b, preferred_element_type=f32)


def mm_t(a, b):
    return lax.dot_general(a, b, (((1,), (1,)), ((), ())), preferred_element_type=f32)


def spread_heads(rows, group):
    if group == 1:
        return rows
    head = lax.broadcasted_iota(jnp.int32, rows.shape, 1) // HEAD_DIM
    zero = jnp.zeros_like(rows)
    return jnp.concatenate([jnp.where(head == h, rows, zero) for h in range(group)], axis=0)


def scores_of(query, key, group, mask, used):
    scores = mm_t(spread_heads(query, group), key)
    if mask is not None:
        scores = jnp.where(mask, scores, NEG)
    if used is not None:
        run = key.shape[0] // 4
        runs = [scores[:, i * run : (i + 1) * run] for i in range(4)]
        scores = jnp.concatenate(runs[:2] + [jnp.where(used > i, runs[i + 1], NEG) for i in (1, 2)], axis=1)
    return scores


def context_of(scores, value, group):
    rows, lanes = scores.shape[0] // group, value.shape[1]
    top = jnp.max(scores, axis=-1, keepdims=True)
    probs = jnp.exp(scores - top).astype(bf16)
    ones = jnp.ones(value.shape, bf16)
    both = mm(probs, jnp.concatenate([value, ones], axis=1))
    head = lax.broadcasted_iota(jnp.int32, (rows, lanes), 1) // HEAD_DIM
    context, total = both[:rows, :lanes], both[:rows, lanes:]
    for h in range(1, group):
        here = both[h * rows : (h + 1) * rows]
        context = jnp.where(head == h, here[:, :lanes], context)
        total = jnp.where(head == h, here[:, lanes:], total)
    return (context / total).astype(bf16)


def attend_all(jobs, ahead):
    ready = [score() for score, _ in jobs[:ahead]]
    for i, (_, finish) in enumerate(jobs):
        if i + ahead < len(jobs):
            ready.append(jobs[i + ahead][0]())
        finish(ready[i])
        ready[i] = None


def whole(shape):
    return pl.BlockSpec(shape, lambda *_: (0,) * len(shape))


def at(index, size):
    return pl.ds(pl.multiple_of(index * size, size), size)


ANY = pl.BlockSpec(memory_space=pl.ANY)


class Plan:
    def __init__(self, axis, devices, steps, block):
        self.axis, self.devices, self.steps, self.block = axis, devices, steps, block
        self.share = devices // steps
        self.half = steps // 2
        self.cells = block // devices
        assert devices % steps == 0 and block % devices == 0

    def place(self):
        me = lax.axis_index(self.axis)
        return me, me // self.share, me % self.share

    def across(self, a, r):
        if r == 0:
            return a
        share = self.share
        pairs = [(i, (i // share ^ r) * share + i % share) for i in range(self.devices)]
        return lax.ppermute(a, self.axis, pairs)

    def within(self, a, d):
        if d == 0:
            return a
        share = self.share
        pairs = [(i, i // share * share + (i % share + d) % share) for i in range(self.devices)]
        return lax.ppermute(a, self.axis, pairs)


def temporal_kernel(plan, nbr_ref, count_ref, frames_ref, gain_ref, wq_ref, wkv_ref, wo_ref, *rest):
    steps = plan.steps
    outs, rows_ref = rest[:-1], rest[-1]
    width = frames_ref.shape[2]
    part = plan.block // 4
    rows = part * steps
    me, slot, _ = plan.place()

    tile = math.gcd(rows, 128)
    r = lax.broadcasted_iota(jnp.int32, (2 * tile, tile), 0) % tile
    c = lax.broadcasted_iota(jnp.int32, (2 * tile, tile), 1)
    mask = (r // steps == c // steps) & (c <= r)

    @pl.loop(0, 4)
    def _(g):
        here = at(g, part)
        wide = frames_ref[here].astype(f32).reshape(rows, width)
        x = normed(wide, gain_ref[...])
        query = (mm(x, wq_ref[...]) * (HEAD_DIM**-0.5)).astype(bf16)
        pairs = mm(x, wkv_ref[...]).astype(bf16)
        parts = {}

        def job(base, lane):
            tiled = slice(base, base + tile)

            def score():
                return scores_of(query[tiled, lane : lane + 128], pairs[tiled, lane : lane + 128], 2, mask, None)

            def finish(scores):
                value = pairs[tiled, width + lane : width + lane + 128]
                parts[base, lane] = context_of(scores, value, 2)

            return score, finish

        spots = [(base, lane) for base in range(0, rows, tile) for lane in range(0, width, 128)]
        attend_all([job(*spot) for spot in spots], AHEAD_T)
        lines = [
            jnp.concatenate([parts[base, lane] for lane in range(0, width, 128)], axis=1)
            for base in range(0, rows, tile)
        ]
        mixed = wide + mm(jnp.concatenate(lines, axis=0), wo_ref[...])
        for lane in range(0, width, 128):
            rows_ref[lane // 128] = mixed[:, lane : lane + 128]
        for peer, out_ref in enumerate(outs):
            when = slot ^ peer
            for lane in range(0, width, 128):
                out_ref[here, lane : lane + 128] = rows_ref[
                    lane // 128, pl.ds(when, part, stride=steps), :
                ].astype(bf16)

    n = plan.devices
    lane = lax.broadcasted_iota(jnp.int32, (NOTE, width), 1)
    note = jnp.where(lane == 0, count_ref[0], 0)
    for i in range(nbr_ref.shape[1]):
        hop = (nbr_ref[0, i] - me + n + n // 2) % n - n // 2
        note = jnp.where(lane == i + 1, hop, note)
    note = note.astype(f32).astype(bf16)
    for out_ref in outs:
        out_ref[plan.block :, :] = note


def temporal(plan, frames, gain, wq, wkv, wo, nbr, count):
    block, steps, width = frames.shape
    messages = [block + NOTE] * steps
    smem = pl.BlockSpec(memory_space=pltpu.SMEM)
    stay = lambda a: pltpu.with_memory_space_constraint(a, pltpu.MemorySpace.HBM)
    arrays = [frames, gain.reshape(1, width), wq, wkv, wo]
    outs = pl.pallas_call(
        functools.partial(temporal_kernel, plan),
        grid=(1,),
        in_specs=[smem, smem] + [whole(a.shape) for a in arrays],
        out_specs=[whole((m, width)) for m in messages],
        scratch_shapes=[pltpu.VMEM((width // 128, block // 4 * steps, 128), f32)],
        out_shape=[jax.ShapeDtypeStruct((m, width), bf16) for m in messages],
        compiler_params=pltpu.CompilerParams(vmem_limit_bytes=24 * MIB),
        cost_estimate=pl.CostEstimate(
            flops=2 * block * steps * width * width * 4, bytes_accessed=6 * MIB, transcendentals=0
        ),
        name="temporal",
    )(nbr, count, *[stay(a) for a in arrays])
    return outs


def project_kernel(plan, labels, stacked, *refs):
    total = 1 if stacked else len(labels)
    ins, rest = refs[:total], refs[total:]
    gain_ref, wq_ref, wkv_ref, q_ref, k_ref, v_ref, x_ref = rest[:7]
    share, half, cells = plan.share, plan.half, plan.cells
    _, slot, member = plan.place()
    part = len(labels) * cells
    width = x_ref.shape[1]
    spots = x_ref.shape[0] // part
    if not stacked:
        spaced_ref = rest[-1]
        for (d, r), piece in zip(labels, ins):
            source = ((slot ^ r) & (half - 1)) * share + (member + share - d) % share
            spaced_ref[:, at(source, cells), :] = piece[: spots * cells, :].astype(f32).reshape(spots, cells, width)
            note = piece[spots * cells :, :128].astype(f32)[:1]
            rest[7][pl.ds(source, 1), :] = note.astype(jnp.int32)
    step = 4
    mine = width // share
    cols = [slice(0, mine), slice(0, mine), slice(mine, 2 * mine)]
    if wq_ref.shape[1] > mine:
        cols = [at(member, mine), at(member, mine), at(share + member, mine)]

    @pl.loop(0, spots // step)
    def _(i):
        here = at(i, step * part)
        if stacked:
            wide = ins[0][here, :].astype(f32)
        else:
            wide = spaced_ref[at(i, step)].reshape(step * part, width)
        x = normed(wide, gain_ref[...])
        q_ref[here, :] = (mm(x, wq_ref[:, cols[0]]) * (HEAD_DIM**-0.5)).astype(bf16)
        k_ref[here, :] = mm(x, wkv_ref[:, cols[1]]).astype(bf16)
        v_ref[here, :] = mm(x, wkv_ref[:, cols[2]]).astype(bf16)
        x_ref[here, :] = wide.astype(bf16)


def project(plan, pieces, gain, weights, after=()):
    labels = list(pieces)
    spots = plan.devices
    ins = [pieces[label] for label in labels]
    width = ins[0].shape[1]
    part = len(labels) * plan.cells
    mine = width // plan.share
    stacked = plan.cells % 8 != 0
    notes = []
    if stacked:
        _, slot, member = plan.place()
        source = jnp.arange(len(labels))
        d = (member + plan.share - source % plan.share) % plan.share
        r = (source // plan.share) ^ (slot & (plan.half - 1))
        pile = jnp.take(jnp.stack(ins), d * plan.half + r, axis=0)
        notes = [pile[:, spots * plan.cells, :128].astype(jnp.int32)]
        rows = pile[:, : spots * plan.cells].reshape(len(labels), spots, plan.cells, width)
        ins = [rows.transpose(1, 0, 2, 3).reshape(spots * part, width)]
    out = [((spots * part, mine), bf16)] * 3 + [((spots * part, width), bf16)]
    if not stacked:
        out.append(((len(labels), 128), jnp.int32))
    arrays = ins + [gain.reshape(1, width)] + list(weights)
    body = functools.partial(project_kernel, plan, labels, stacked)
    outs = pl.pallas_call(
        lambda *refs: body(*refs[len(after) :]),
        grid=(1,),
        in_specs=[ANY] * len(after) + [whole(a.shape) for a in arrays],
        out_specs=[whole(o) for o, _ in out],
        scratch_shapes=[] if stacked else [pltpu.VMEM((spots, part, width), f32)],
        out_shape=[jax.ShapeDtypeStruct(o, t) for o, t in out],
        compiler_params=pltpu.CompilerParams(vmem_limit_bytes=24 * MIB),
        cost_estimate=pl.CostEstimate(
            flops=2 * spots * part * width * mine * 3, bytes_accessed=4 * MIB, transcendentals=0
        ),
        name="project",
    )(*after, *arrays)
    return outs[:3], outs[3], (notes or outs[4:])


def spatial_kernel(plan, peers, notes_ref, *rest):
    share, block, n = plan.share, plan.block, plan.devices
    early, late, outs = rest[:3], rest[3:6], rest[6:]
    _, slot, member = plan.place()
    width = outs[0].shape[1]
    group = min(2, width // HEAD_DIM)
    lanes = group * HEAD_DIM
    part = block // 2

    def rows(which, b, cols):
        return [early[which][at(b, part), cols], late[which][at(b, part), cols]]

    def job(i, d, lane):
        b = (slot ^ peers[i]) * share + (member + d) % share
        note = b % (n // 2)
        blocks = [b] + [(b + notes_ref[note, 1 + k] + n) % n for k in range(3)]
        cols = slice(lane, lane + lanes)

        def score():
            key = jnp.concatenate([p for k in blocks for p in rows(1, k, cols)], axis=0)
            return scores_of(jnp.concatenate(rows(0, b, cols), axis=0), key, group, None, notes_ref[note, 0])

        def finish(scores):
            value = jnp.concatenate([p for k in blocks for p in rows(2, k, cols)], axis=0)
            outs[d][i * block : (i + 1) * block, cols] = context_of(scores, value, group)

        return score, finish

    spots = [(i, d, lane) for d in reversed(range(share)) for i in range(len(peers)) for lane in range(0, width, lanes)]
    attend_all([job(*spot) for spot in spots], AHEAD_S)


def spatial(plan, notes, sets, peers, after=()):
    block, share = plan.block, plan.share
    mine = sets[0][0].shape[1]
    out = (len(peers) * block, mine)
    arrays = [a for trio in sets for a in trio]
    body = functools.partial(spatial_kernel, plan, peers)
    return pl.pallas_call(
        lambda notes_ref, *refs: body(notes_ref, *refs[len(after) :]),
        grid_spec=pltpu.PrefetchScalarGridSpec(
            num_scalar_prefetch=1,
            grid=(1,),
            in_specs=[ANY] * len(after) + [whole(a.shape) for a in arrays],
            out_specs=[whole(out)] * share,
        ),
        out_shape=[jax.ShapeDtypeStruct(out, bf16)] * share,
        compiler_params=pltpu.CompilerParams(vmem_limit_bytes=24 * MIB),
        cost_estimate=pl.CostEstimate(
            flops=4 * 2 * share * len(peers) * block * block * 4 * mine, bytes_accessed=3 * MIB, transcendentals=0
        ),
        name="spatial",
    )(notes, *after, *arrays)


def dense_kernel(plan, peers, *refs):
    share, block = plan.share, plan.block
    contexts, rest = refs[:share], refs[share:]
    x_refs, rest = rest[:2], rest[2:]
    gain_ref, wo_ref, gate_ref, up_ref, down_ref = rest[:5]
    outs = rest[5:]
    _, slot, member = plan.place()
    mine = contexts[0].shape[1]
    part = block // 2
    pieces = []
    for r in peers:
        b = (slot ^ r) * share + member
        pieces += [x_ref[at(b, part), :].astype(f32) for x_ref in x_refs]
    after = jnp.concatenate(pieces, axis=0)
    for d in range(share):
        source = (member + share - d) % share
        after += mm(contexts[d][...], wo_ref[at(source, mine), :])
    after = after.astype(bf16).astype(f32)
    x = normed(after, gain_ref[...])
    chunk = 512
    total = after
    for start in range(0, gate_ref.shape[1], chunk):
        gate = mm(x, gate_ref[:, start : start + chunk])
        up = mm(x, up_ref[:, start : start + chunk])
        hidden = (gate / (1.0 + jnp.exp(-gate)) * up).astype(bf16)
        total += mm(hidden, down_ref[start : start + chunk, :])
    for k, out_ref in enumerate(outs):
        out_ref[...] = total[k * block : (k + 1) * block].astype(bf16)


def dense(plan, contexts, xs, peers, gain, wo, gate, up, down, after=()):
    rows = contexts[0].shape[0]
    width = xs[0].shape[1]
    arrays = list(contexts) + list(xs) + [gain.reshape(1, width), wo, gate, up, down]
    body = functools.partial(dense_kernel, plan, peers)
    out = jax.ShapeDtypeStruct((plan.block, width), bf16)
    return pl.pallas_call(
        lambda *refs: body(*refs[len(after) :]),
        grid=(1,),
        in_specs=[ANY] * len(after) + [whole(a.shape) for a in arrays],
        out_specs=[whole(out.shape)] * len(peers),
        out_shape=[out] * len(peers),
        compiler_params=pltpu.CompilerParams(vmem_limit_bytes=24 * MIB),
        cost_estimate=pl.CostEstimate(
            flops=2 * rows * width * (width + 3 * gate.shape[1]), bytes_accessed=8 * MIB, transcendentals=0
        ),
        name="dense",
    )(*after, *arrays)


def gather_kernel(plan, *refs):
    ins, out_ref, rows_ref = refs[:-2], refs[-2], refs[-1]
    steps, block = plan.steps, plan.block
    part = block // 2
    _, slot, _ = plan.place()
    for lane in range(0, out_ref.shape[2], 128):
        cols = slice(lane, lane + 128)
        for r in range(steps):
            when = slot ^ r
            early = jnp.where(when >= plan.half, part * steps, 0)
            for k in range(2):
                start = (part * steps - early if k else early) + when
                rows_ref[lane // 128, pl.ds(start, part, stride=steps), :] = ins[r][
                    k * part : (k + 1) * part, cols
                ].astype(f32)
        out_ref[:, :, cols] = rows_ref[lane // 128].reshape(block, steps, 128).astype(bf16)


def gather(plan, pieces):
    block, width = pieces[0].shape
    steps = plan.steps
    return pl.pallas_call(
        functools.partial(gather_kernel, plan),
        out_shape=jax.ShapeDtypeStruct((block, steps, width), bf16),
        scratch_shapes=[pltpu.VMEM((width // 128, block * steps, 128), f32)],
        compiler_params=pltpu.CompilerParams(vmem_limit_bytes=16 * MIB),
        cost_estimate=pl.CostEstimate(flops=MIB, bytes_accessed=2 * MIB, transcendentals=0),
        name="gather",
    )(*pieces)


def layer(
    frames, norm_time, t_wq, t_wkv, t_wo, norm_space, s_wq, s_wkv, s_wo, norm_mlp, w_gate, w_up, w_down,
    nbr_blocks, nbr_count,
):
    block, steps, width = frames.shape
    plan = Plan("cell", lax.axis_size("cell"), steps, block)
    half, share = plan.half, plan.share
    mine = width // share
    weights = [s_wq, s_wkv]
    if mine % 128:
        member = lax.axis_index("cell") % share
        take = lambda w, start: lax.dynamic_slice_in_dim(w, start * width + member * mine, mine, axis=1)
        weights = [take(s_wq, 0), jnp.concatenate([take(s_wkv, 0), take(s_wkv, 1)], axis=1)]

    def send(a, r):
        return plan.across(a, r)

    sent = temporal(plan, frames, norm_time, t_wq, t_wkv, t_wo, nbr_blocks, nbr_count)
    got = {r: send(sent[r], r) for r in reversed(range(steps))}

    def shared(peers):
        return {(d, r): plan.within(got[r], d) for d in range(share) for r in peers}

    early, x_early, (notes_early,) = project(plan, shared(range(half)), norm_space, weights)
    late, x_late, (notes_late,) = project(plan, shared(range(half, steps)), norm_space, weights, (x_early,))

    each = steps // PIECES
    peers = [tuple(range(i * each, (i + 1) * each)) for i in range(PIECES)][::-1]
    mlp = (norm_mlp, s_wo, w_gate, w_up, w_down)
    landed = [None] * steps

    def scores(i, after):
        notes = notes_late if peers[i][0] >= half else notes_early
        raw = spatial(plan, notes, (early, late), peers[i], after)
        return [plan.within(c, d) for d, c in enumerate(raw)], (raw[0],)

    def finish(i, contexts, after):
        outs = dense(plan, contexts, (x_early, x_late), peers[i], *mlp, after=after)
        for r, out in zip(peers[i], outs):
            landed[r] = send(out, r)
        return (outs[0],)

    c0, last = scores(0, ())
    last = finish(0, c0, last)
    c1, last = scores(1, last)
    c2, last = scores(2, last)
    last = finish(1, c1, last)
    c3, last = scores(3, last)
    last = finish(2, c2, last)
    finish(3, c3, last)
    return gather(plan, landed)


def solution(mesh):
    rows = P(("groups", "cell"))
    placed = (rows,) + (P(),) * 12 + (rows, rows)
    return jax.shard_map(layer, mesh=mesh, in_specs=placed, out_specs=rows, check_vma=False)
```

profile of v0, /device:TPU:1, one launch (start us, length us, event | category | flops | bytes accessed | tf_op | source)
XLA Modules:
  0.0 85.6 jit_solution(2065651049216678236)
XLA Ops:
  0.7 0.6 copy-done.8
  1.3 7.8 %temporal.1 = (bf16[136,512]{1,0:T(8,128)(2,1)S(1)}, bf16[136,512]{1,0:T(8,128)(2,1)S(1)}, bf16[136,512]{1,0:T(8,128)(2,1)S(1)}, bf16[136,512]{1,0:T(8,128)(2,1)...) custom-call(s32[1,3]{1,0:T(1,128)S(1)} %copy-done.8, ...), custom_call_target="tpu_custom_call" | custom-call | flops 2147483648 | bytes 6291456 | tf_op jit(solution)/shard_map/temporal/pallas_call | solution.py:186
  9.1 2.1 %collective-permute-start = (bf16[136,512]{1,0:T(8,128)(2,1)S(1)}, bf16[136,512]{1,0:T(8,128)(2,1)S(1)}, u32[]{:S(2)}, u32[]{:S(2)}) collective-permute-start(bf16[136,512]{1,0:T(8,128)(2,1)S(1)} %get-tuple-element.40), channel_id=1, source_target_pairs={{0,2},{1,3},{2,0},{3,1},{4,6},{5,7},{6,4},{7,5},{8,10},{9,11},{10,... | collective-permute-start | bytes 417800 | tf_op jit(solution)/shard_map/ppermute | solution.py:109
  11.3 1.3 %collective-permute-start.1 = (bf16[136,512]{1,0:T(8,128)(2,1)S(1)}, bf16[136,512]{1,0:T(8,128)(2,1)S(1)}, u32[]{:S(2)}, u32[]{:S(2)}) collective-permute-start(bf16[136,512]{1,0:T(8,128)(2,1)S(1)} %get-tuple-element.41), channel_id=1, source_target_pairs={{0,4},{1,5},{2,6},{3,7},{4,0},{5,1},{6,2},{7,3},{8,12},{9,13},{10,... | collective-permute-start | bytes 417800 | tf_op jit(solution)/shard_map/ppermute | solution.py:109
  12.6 2.4 %collective-permute-start.7 = (bf16[136,512]{1,0:T(8,128)(2,1)S(1)}, bf16[136,512]{1,0:T(8,128)(2,1)S(1)}, u32[]{:S(2)}, u32[]{:S(2)}) collective-permute-start(bf16[136,512]{1,0:T(8,128)(2,1)S(1)} %get-tuple-element.45), channel_id=1, source_target_pairs={{0,8},{1,9},{2,10},{3,11},{4,12},{5,13},{6,14},{7,15},{8,0},{9,1},... | collective-permute-start | bytes 417800 | tf_op jit(solution)/shard_map/ppermute | solution.py:109
  15.0 1.0 %collective-permute-start.8 = (bf16[136,512]{1,0:T(8,128)(2,1)S(1)}, bf16[136,512]{1,0:T(8,128)(2,1)S(1)}, u32[]{:S(2)}, u32[]{:S(2)}) collective-permute-start(bf16[136,512]{1,0:T(8,128)(2,1)S(1)} %get-tuple-element.46), channel_id=1, source_target_pairs={{0,10},{1,11},{2,8},{3,9},{4,14},{5,15},{6,12},{7,13},{8,2},{9,3},... | collective-permute-start | bytes 417800 | tf_op jit(solution)/shard_map/ppermute | solution.py:109
  16.0 3.3 %collective-permute-start.9 = (bf16[136,512]{1,0:T(8,128)(2,1)S(1)}, bf16[136,512]{1,0:T(8,128)(2,1)S(1)}, u32[]{:S(2)}, u32[]{:S(2)}) collective-permute-start(bf16[136,512]{1,0:T(8,128)(2,1)S(1)} %get-tuple-element.47), channel_id=1, source_target_pairs={{0,12},{1,13},{2,14},{3,15},{4,8},{5,9},{6,10},{7,11},{8,4},{9,5},... | collective-permute-start | bytes 417800 | tf_op jit(solution)/shard_map/ppermute | solution.py:109
  19.3 0.0 collective-permute-start.10
  19.3 4.1 %collective-permute-done.2.refs_3_ = bf16[136,512]{1,0:T(8,128)(2,1)S(1)} collective-permute-done((bf16[136,512]{1,0:T(8,128)(2,1)S(1)}, bf16[136,512]{1,0:T(8,128)(2,1)S(1)}, u32[]{:S(2)}, u32[]{:S(2)}) %collective-permute-start.2) | collective-permute-done | bytes 139296 | tf_op jit(solution)/shard_map/ppermute | solution.py:109
  23.4 1.0 %collective-permute-start.3 = (bf16[136,512]{1,0:T(8,128)(2,1)S(1)}, bf16[136,512]{1,0:T(8,128)(2,1)S(1)}, u32[]{:S(2)}, u32[]{:S(2)}) collective-permute-start(bf16[136,512]{1,0:T(8,128)(2,1)S(1)} %get-tuple-element.39.refs_0_), channel_id=1, source_target_pairs={{0,1},{1,0},{2,3},{3,2},{4,5},{5,4},{6,7},{7,6},{8,9},{9,8},{10,11... | collective-permute-start | bytes 417800 | tf_op jit(solution)/shard_map/ppermute | solution.py:116
  24.4 0.0 collective-permute-start.4
  24.4 10.0 %collective-permute-done.8.refs_2_ = bf16[136,512]{1,0:T(8,128)(2,1)S(1)} collective-permute-done((bf16[136,512]{1,0:T(8,128)(2,1)S(1)}, bf16[136,512]{1,0:T(8,128)(2,1)S(1)}, u32[]{:S(2)}, u32[]{:S(2)}) %collective-permute-start.8) | collective-permute-done | bytes 139296 | tf_op jit(solution)/shard_map/ppermute | solution.py:109
  34.4 2.9 %collective-permute-start.5 = (bf16[136,512]{1,0:T(8,128)(2,1)S(1)}, bf16[136,512]{1,0:T(8,128)(2,1)S(1)}, u32[]{:S(2)}, u32[]{:S(2)}) collective-permute-start(bf16[136,512]{1,0:T(8,128)(2,1)S(1)} %collective-permute-done.1.refs_2_), channel_id=1, source_target_pairs={{0,1},{1,0},{2,3},{3,2},{4,5},{5,4},{6,7},{7,6},{8,9},{9,8},{10,11... | collective-permute-start | bytes 417800 | tf_op jit(solution)/shard_map/ppermute | solution.py:116
  37.3 0.0 collective-permute-start.6
  37.3 0.5 collective-permute-start.11
  37.8 0.1 collective-permute-start.12
  37.9 0.4 collective-permute-start.13
  38.3 0.3 collective-permute-start.14
  38.6 1.9 %project.2 = (bf16[1024,256]{1,0:T(8,128)(2,1)S(1)}, bf16[1024,256]{1,0:T(8,128)(2,1)S(1)}, bf16[1024,256]{1,0:T(8,128)(2,1)S(1)}, bf16[1024,512]{1,0:T(8,128)(2,1)S(1)}, s32[8,128]{1,0:T(8,128)S(1)}) custom-call(bf16[136,512]{1,0:T(8,128)(2,1)S(1)} %get-tuple-element.39.refs_0_, bf16[136,512]{1,0:T(8,128)(2,1)S(1)} %collective-permute-done.refs_1_, ...), custom_call_target="tpu_custom_call" | custom-call | flops 805306368 | bytes 4194304 | tf_op jit(solution)/shard_map/project/pallas_call | solution.py:261
  40.6 0.0 copy-start.1
  40.6 0.0 copy-start.2
  40.7 2.1 %project.3 = (bf16[1024,256]{1,0:T(8,128)(2,1)S(1)}, bf16[1024,256]{1,0:T(8,128)(2,1)S(1)}, bf16[1024,256]{1,0:T(8,128)(2,1)S(1)}, bf16[1024,512]{1,0:T(8,128)(2,1)S(1)}, s32[8,128]{1,0:T(8,128)S(1)}) custom-call(bf16[1024,512]{1,0:T(8,128)(2,1)S(1)} %get-tuple-element.44.refs_0_.refs_3_, bf16[136,512]{1,0:T(8,128)(2,1)S(1)} %collective-permute-done.7.refs_1_, ...), custom_call_target="tpu_custom_call" | custom-call | flops 805306368 | bytes 4194304 | tf_op jit(solution)/shard_map/project/pallas_call | solution.py:261
  42.8 0.0 copy-start
  42.8 0.0 copy-start.3
  42.8 2.1 %spatial.4 = (bf16[256,256]{1,0:T(8,128)(2,1)S(1)}, bf16[256,256]{1,0:T(8,128)(2,1)S(1)}) custom-call(s32[8,128]{1,0:T(8,128)S(1)} %get-tuple-element.49.notes_ref, bf16[1024,256]{1,0:T(8,128)(2,1)S(1)} %get-tuple-element.50.refs_0_.refs_1_, bf16[1024,256]{1,0:T(8,128)(2,1)S(1)} %get-tuple-element.51.refs_1_.refs_2_, ...), custom_call_target="tpu_custom_call" | custom-call | flops 536870912 | bytes 3145728 | tf_op jit(solution)/shard_map/spatial/pallas_call | solution.py:315
  45.0 0.2 collective-permute-start.15
  45.2 1.2 %collective-permute-done.15.refs_2_ = bf16[256,256]{1,0:T(8,128)(2,1)S(1)} collective-permute-done((bf16[256,256]{1,0:T(8,128)(2,1)S(1)}, bf16[256,256]{1,0:T(8,128)(2,1)S(1)}, u32[]{:S(2)}, u32[]{:S(2)}) %collective-permute-start.15) | collective-permute-done | bytes 131104 | tf_op jit(solution)/shard_map/ppermute | solution.py:116
  46.4 2.6 %dense.4 = (bf16[128,512]{1,0:T(8,128)(2,1)S(1)}, bf16[128,512]{1,0:T(8,128)(2,1)S(1)}) custom-call(bf16[256,256]{1,0:T(8,128)(2,1)S(1)} %get-tuple-element.56.refs_0_.refs_1_, bf16[256,256]{1,0:T(8,128)(2,1)S(1)} %get-tuple-element.56.refs_0_.refs_1_, bf16[256,256]{1,0:T(8,128)(2,1)S(1)} %collective-permute-done.15.refs_2_, ...), custom_call_target="tpu_custom_call" | custom-call | flops 1744830464 | bytes 8388608 | tf_op jit(solution)/shard_map/dense/pallas_call | solution.py:368
  49.0 2.1 %spatial.5 = (bf16[256,256]{1,0:T(8,128)(2,1)S(1)}, bf16[256,256]{1,0:T(8,128)(2,1)S(1)}) custom-call(s32[8,128]{1,0:T(8,128)S(1)} %get-tuple-element.49.notes_ref, bf16[128,512]{1,0:T(8,128)(2,1)S(1)} %get-tuple-element.59.refs_0_, bf16[1024,256]{1,0:T(8,128)(2,1)S(1)} %get-tuple-element.50.refs_0_.refs_1_, ...), custom_call_target="tpu_custom_call" | custom-call | flops 536870912 | bytes 3145728 | tf_op jit(solution)/shard_map/spatial/pallas_call | solution.py:315
  51.2 0.2 collective-permute-start.16
  51.4 3.1 %collective-permute-start.24 = (bf16[128,512]{1,0:T(8,128)(2,1)S(1)}, bf16[128,512]{1,0:T(8,128)(2,1)S(1)}, u32[]{:S(2)}, u32[]{:S(2)}) collective-permute-start(bf16[128,512]{1,0:T(8,128)(2,1)S(1)} %get-tuple-element.59.refs_0_), channel_id=1, source_target_pairs={{0,12},{1,13},{2,14},{3,15},{4,8},{5,9},{6,10},{7,11},{8,4},{9,5},... | collective-permute-start | bytes 393224 | tf_op jit(solution)/shard_map/ppermute | solution.py:109
  54.5 0.5 collective-permute-start.25
  54.9 2.1 %spatial.6 = (bf16[256,256]{1,0:T(8,128)(2,1)S(1)}, bf16[256,256]{1,0:T(8,128)(2,1)S(1)}) custom-call(s32[8,128]{1,0:T(8,128)S(1)} %get-tuple-element.43.notes_ref, bf16[256,256]{1,0:T(8,128)(2,1)S(1)} %get-tuple-element.60.refs_0_.refs_1_, bf16[1024,256]{1,0:T(8,128)(2,1)S(1)} %get-tuple-element.50.refs_0_.refs_1_, ...), custom_call_target="tpu_custom_call" | custom-call | flops 536870912 | bytes 3145728 | tf_op jit(solution)/shard_map/spatial/pallas_call | solution.py:315
  57.1 0.9 %collective-permute-start.17 = (bf16[256,256]{1,0:T(8,128)(2,1)S(1)}, bf16[256,256]{1,0:T(8,128)(2,1)S(1)}, u32[]{:S(2)}, u32[]{:S(2)}) collective-permute-start(bf16[256,256]{1,0:T(8,128)(2,1)S(1)} %get-tuple-element.65), channel_id=1, source_target_pairs={{0,1},{1,0},{2,3},{3,2},{4,5},{5,4},{6,7},{7,6},{8,9},{9,8},{10,11... | collective-permute-start | bytes 393224 | tf_op jit(solution)/shard_map/ppermute | solution.py:116
  57.9 2.6 %dense.5 = (bf16[128,512]{1,0:T(8,128)(2,1)S(1)}, bf16[128,512]{1,0:T(8,128)(2,1)S(1)}) custom-call(bf16[256,256]{1,0:T(8,128)(2,1)S(1)} %get-tuple-element.61.refs_0_.refs_1_, bf16[256,256]{1,0:T(8,128)(2,1)S(1)} %get-tuple-element.60.refs_0_.refs_1_, bf16[256,256]{1,0:T(8,128)(2,1)S(1)} %collective-permute-done.16.refs_2_, ...), custom_call_target="tpu_custom_call" | custom-call | flops 1744830464 | bytes 8388608 | tf_op jit(solution)/shard_map/dense/pallas_call | solution.py:368
  60.6 4.1 %collective-permute-start.22 = (bf16[128,512]{1,0:T(8,128)(2,1)S(1)}, bf16[128,512]{1,0:T(8,128)(2,1)S(1)}, u32[]{:S(2)}, u32[]{:S(2)}) collective-permute-start(bf16[128,512]{1,0:T(8,128)(2,1)S(1)} %get-tuple-element.63.refs_0_), channel_id=1, source_target_pairs={{0,8},{1,9},{2,10},{3,11},{4,12},{5,13},{6,14},{7,15},{8,0},{9,1},... | collective-permute-start | bytes 393224 | tf_op jit(solution)/shard_map/ppermute | solution.py:109
  64.6 2.1 %spatial.7 = (bf16[256,256]{1,0:T(8,128)(2,1)S(1)}, bf16[256,256]{1,0:T(8,128)(2,1)S(1)}) custom-call(s32[8,128]{1,0:T(8,128)S(1)} %get-tuple-element.43.notes_ref, bf16[128,512]{1,0:T(8,128)(2,1)S(1)} %get-tuple-element.63.refs_0_, bf16[1024,256]{1,0:T(8,128)(2,1)S(1)} %get-tuple-element.50.refs_0_.refs_1_, ...), custom_call_target="tpu_custom_call" | custom-call | flops 536870912 | bytes 3145728 | tf_op jit(solution)/shard_map/spatial/pallas_call | solution.py:315
  66.8 0.4 collective-permute-start.18
  67.2 0.7 collective-permute-start.23
  67.9 2.6 %dense.6 = (bf16[128,512]{1,0:T(8,128)(2,1)S(1)}, bf16[128,512]{1,0:T(8,128)(2,1)S(1)}) custom-call(bf16[256,256]{1,0:T(8,128)(2,1)S(1)} %get-tuple-element.64.refs_0_.refs_1_, bf16[256,256]{1,0:T(8,128)(2,1)S(1)} %get-tuple-element.61.refs_0_.refs_1_, bf16[256,256]{1,0:T(8,128)(2,1)S(1)} %collective-permute-done.17.refs_2_, ...), custom_call_target="tpu_custom_call" | custom-call | flops 1744830464 | bytes 8388608 | tf_op jit(solution)/shard_map/dense/pallas_call | solution.py:368
  70.5 1.2 %collective-permute-start.20 = (bf16[128,512]{1,0:T(8,128)(2,1)S(1)}, bf16[128,512]{1,0:T(8,128)(2,1)S(1)}, u32[]{:S(2)}, u32[]{:S(2)}) collective-permute-start(bf16[128,512]{1,0:T(8,128)(2,1)S(1)} %get-tuple-element.66.refs_0_), channel_id=1, source_target_pairs={{0,4},{1,5},{2,6},{3,7},{4,0},{5,1},{6,2},{7,3},{8,12},{9,13},{10,... | collective-permute-start | bytes 393224 | tf_op jit(solution)/shard_map/ppermute | solution.py:109
  71.7 2.6 %dense.7 = (bf16[128,512]{1,0:T(8,128)(2,1)S(1)}, bf16[128,512]{1,0:T(8,128)(2,1)S(1)}) custom-call(bf16[128,512]{1,0:T(8,128)(2,1)S(1)} %get-tuple-element.66.refs_0_, bf16[256,256]{1,0:T(8,128)(2,1)S(1)} %get-tuple-element.64.refs_0_.refs_1_, bf16[256,256]{1,0:T(8,128)(2,1)S(1)} %collective-permute-done.18.refs_2_, ...), custom_call_target="tpu_custom_call" | custom-call | flops 1744830464 | bytes 8388608 | tf_op jit(solution)/shard_map/dense/pallas_call | solution.py:368
  74.4 0.6 collective-permute-start.21
  74.9 1.0 %collective-permute-start.19 = (bf16[128,512]{1,0:T(8,128)(2,1)S(1)}, bf16[128,512]{1,0:T(8,128)(2,1)S(1)}, u32[]{:S(2)}, u32[]{:S(2)}) collective-permute-start(bf16[128,512]{1,0:T(8,128)(2,1)S(1)} %get-tuple-element.69), channel_id=1, source_target_pairs={{0,2},{1,3},{2,0},{3,1},{4,6},{5,7},{6,4},{7,5},{8,10},{9,11},{10,... | collective-permute-start | bytes 393224 | tf_op jit(solution)/shard_map/ppermute | solution.py:109
  75.9 2.6 %collective-permute-done.23.refs_5_ = bf16[128,512]{1,0:T(8,128)(2,1)S(1)} collective-permute-done((bf16[128,512]{1,0:T(8,128)(2,1)S(1)}, bf16[128,512]{1,0:T(8,128)(2,1)S(1)}, u32[]{:S(2)}, u32[]{:S(2)}) %collective-permute-start.23) | collective-permute-done | bytes 131104 | tf_op jit(solution)/shard_map/ppermute | solution.py:109
  78.5 4.7 %collective-permute-done.21.refs_3_ = bf16[128,512]{1,0:T(8,128)(2,1)S(1)} collective-permute-done((bf16[128,512]{1,0:T(8,128)(2,1)S(1)}, bf16[128,512]{1,0:T(8,128)(2,1)S(1)}, u32[]{:S(2)}, u32[]{:S(2)}) %collective-permute-start.21) | collective-permute-done | bytes 131104 | tf_op jit(solution)/shard_map/ppermute | solution.py:109
  83.3 0.7 collective-permute-done.19.refs_1_
  83.9 1.7 %gather.1 = bf16[128,8,512]{2,1,0:T(8,128)(2,1)} custom-call(bf16[128,512]{1,0:T(8,128)(2,1)S(1)} %get-tuple-element.68.refs_0_, bf16[128,512]{1,0:T(8,128)(2,1)S(1)} %collective-permute-done.19.refs_1_, bf16[128,512]{1,0:T(8,128)(2,1)S(1)} %collective-permute-done.20.refs_2_, bf16[128,512]{1,0:T(8,128)(2,1)S(1)} %collective-permute-done.21.refs_3_, ...), custom_call_target="tpu_custom_call" | custom-call | flops 1048576 | bytes 2097152 | tf_op jit(solution)/shard_map/gather/pallas_call | solution.py:403
  (34 shorter events, 0.1 us)
Async XLA Ops:
  0.7 0.7 copy-start.8
  1.3 37.3 %copy-start.4 = (bf16[512,1024]{1,0:T(8,128)(2,1)S(1)}, bf16[512,1024]{1,0:T(8,128)(2,1)}, u32[]{:S(2)}) copy-start(bf16[512,1024]{1,0:T(8,128)(2,1)} %refs_11_.1) | copy-start | bytes 3145732
  1.3 37.3 %copy-start.5 = (bf16[512,512]{1,0:T(8,128)(2,1)S(1)}, bf16[512,512]{1,0:T(8,128)(2,1)}, u32[]{:S(2)}) copy-start(bf16[512,512]{1,0:T(8,128)(2,1)} %refs_10_.3) | copy-start | bytes 1572868
  1.3 37.3 %copy-start.7 = (f32[512]{0:T(512)S(1)}, f32[512]{0:T(512)}, u32[]{:S(2)}) copy-start(f32[512]{0:T(512)} %param.20) | copy-start | bytes 6148
  9.1 6.9 %collective-permute-start = (bf16[136,512]{1,0:T(8,128)(2,1)S(1)}, bf16[136,512]{1,0:T(8,128)(2,1)S(1)}, u32[]{:S(2)}, u32[]{:S(2)}) collective-permute-start(bf16[136,512]{1,0:T(8,128)(2,1)S(1)} %get-tuple-element.40), channel_id=1, source_target_pairs={{0,2},{1,3},{2,0},{3,1},{4,6},{5,7},{6,4},{7,5},{8,10},{9,11},{10,... | collective-permute-start | bytes 417800 | tf_op jit(solution)/shard_map/ppermute | solution.py:109
  11.3 8.0 %collective-permute-start.1 = (bf16[136,512]{1,0:T(8,128)(2,1)S(1)}, bf16[136,512]{1,0:T(8,128)(2,1)S(1)}, u32[]{:S(2)}, u32[]{:S(2)}) collective-permute-start(bf16[136,512]{1,0:T(8,128)(2,1)S(1)} %get-tuple-element.41), channel_id=1, source_target_pairs={{0,4},{1,5},{2,6},{3,7},{4,0},{5,1},{6,2},{7,3},{8,12},{9,13},{10,... | collective-permute-start | bytes 417800 | tf_op jit(solution)/shard_map/ppermute | solution.py:109
  12.6 10.9 %collective-permute-start.2 = (bf16[136,512]{1,0:T(8,128)(2,1)S(1)}, bf16[136,512]{1,0:T(8,128)(2,1)S(1)}, u32[]{:S(2)}, u32[]{:S(2)}) collective-permute-start(bf16[136,512]{1,0:T(8,128)(2,1)S(1)} %get-tuple-element.42), channel_id=1, source_target_pairs={{0,6},{1,7},{2,4},{3,5},{4,2},{5,3},{6,0},{7,1},{8,14},{9,15},{10,... | collective-permute-start | bytes 417800 | tf_op jit(solution)/shard_map/ppermute | solution.py:109
  12.6 11.9 %collective-permute-start.7 = (bf16[136,512]{1,0:T(8,128)(2,1)S(1)}, bf16[136,512]{1,0:T(8,128)(2,1)S(1)}, u32[]{:S(2)}, u32[]{:S(2)}) collective-permute-start(bf16[136,512]{1,0:T(8,128)(2,1)S(1)} %get-tuple-element.45), channel_id=1, source_target_pairs={{0,8},{1,9},{2,10},{3,11},{4,12},{5,13},{6,14},{7,15},{8,0},{9,1},... | collective-permute-start | bytes 417800 | tf_op jit(solution)/shard_map/ppermute | solution.py:109
  15.0 19.4 %collective-permute-start.8 = (bf16[136,512]{1,0:T(8,128)(2,1)S(1)}, bf16[136,512]{1,0:T(8,128)(2,1)S(1)}, u32[]{:S(2)}, u32[]{:S(2)}) collective-permute-start(bf16[136,512]{1,0:T(8,128)(2,1)S(1)} %get-tuple-element.46), channel_id=1, source_target_pairs={{0,10},{1,11},{2,8},{3,9},{4,14},{5,15},{6,12},{7,13},{8,2},{9,3},... | collective-permute-start | bytes 417800 | tf_op jit(solution)/shard_map/ppermute | solution.py:109
  16.0 21.3 %collective-permute-start.9 = (bf16[136,512]{1,0:T(8,128)(2,1)S(1)}, bf16[136,512]{1,0:T(8,128)(2,1)S(1)}, u32[]{:S(2)}, u32[]{:S(2)}) collective-permute-start(bf16[136,512]{1,0:T(8,128)(2,1)S(1)} %get-tuple-element.47), channel_id=1, source_target_pairs={{0,12},{1,13},{2,14},{3,15},{4,8},{5,9},{6,10},{7,11},{8,4},{9,5},... | collective-permute-start | bytes 417800 | tf_op jit(solution)/shard_map/ppermute | solution.py:109
  19.3 18.0 %collective-permute-start.10 = (bf16[136,512]{1,0:T(8,128)(2,1)S(1)}, bf16[136,512]{1,0:T(8,128)(2,1)S(1)}, u32[]{:S(2)}, u32[]{:S(2)}) collective-permute-start(bf16[136,512]{1,0:T(8,128)(2,1)S(1)} %get-tuple-element.48), channel_id=1, source_target_pairs={{0,14},{1,15},{2,12},{3,13},{4,10},{5,11},{6,8},{7,9},{8,6},{9,7},... | collective-permute-start | bytes 417800 | tf_op jit(solution)/shard_map/ppermute | solution.py:109
  23.4 14.4 %collective-permute-start.3 = (bf16[136,512]{1,0:T(8,128)(2,1)S(1)}, bf16[136,512]{1,0:T(8,128)(2,1)S(1)}, u32[]{:S(2)}, u32[]{:S(2)}) collective-permute-start(bf16[136,512]{1,0:T(8,128)(2,1)S(1)} %get-tuple-element.39.refs_0_), channel_id=1, source_target_pairs={{0,1},{1,0},{2,3},{3,2},{4,5},{5,4},{6,7},{7,6},{8,9},{9,8},{10,11... | collective-permute-start | bytes 417800 | tf_op jit(solution)/shard_map/ppermute | solution.py:116
  24.4 13.4 %collective-permute-start.4 = (bf16[136,512]{1,0:T(8,128)(2,1)S(1)}, bf16[136,512]{1,0:T(8,128)(2,1)S(1)}, u32[]{:S(2)}, u32[]{:S(2)}) collective-permute-start(bf16[136,512]{1,0:T(8,128)(2,1)S(1)} %collective-permute-done.refs_1_), channel_id=1, source_target_pairs={{0,1},{1,0},{2,3},{3,2},{4,5},{5,4},{6,7},{7,6},{8,9},{9,8},{10,11... | collective-permute-start | bytes 417800 | tf_op jit(solution)/shard_map/ppermute | solution.py:116
  34.4 3.9 %collective-permute-start.5 = (bf16[136,512]{1,0:T(8,128)(2,1)S(1)}, bf16[136,512]{1,0:T(8,128)(2,1)S(1)}, u32[]{:S(2)}, u32[]{:S(2)}) collective-permute-start(bf16[136,512]{1,0:T(8,128)(2,1)S(1)} %collective-permute-done.1.refs_2_), channel_id=1, source_target_pairs={{0,1},{1,0},{2,3},{3,2},{4,5},{5,4},{6,7},{7,6},{8,9},{9,8},{10,11... | collective-permute-start | bytes 417800 | tf_op jit(solution)/shard_map/ppermute | solution.py:116
  37.3 1.4 %collective-permute-start.6 = (bf16[136,512]{1,0:T(8,128)(2,1)S(1)}, bf16[136,512]{1,0:T(8,128)(2,1)S(1)}, u32[]{:S(2)}, u32[]{:S(2)}) collective-permute-start(bf16[136,512]{1,0:T(8,128)(2,1)S(1)} %collective-permute-done.2.refs_3_), channel_id=1, source_target_pairs={{0,1},{1,0},{2,3},{3,2},{4,5},{5,4},{6,7},{7,6},{8,9},{9,8},{10,11... | collective-permute-start | bytes 417800 | tf_op jit(solution)/shard_map/ppermute | solution.py:116
  37.3 3.3 %collective-permute-start.11 = (bf16[136,512]{1,0:T(8,128)(2,1)S(1)}, bf16[136,512]{1,0:T(8,128)(2,1)S(1)}, u32[]{:S(2)}, u32[]{:S(2)}) collective-permute-start(bf16[136,512]{1,0:T(8,128)(2,1)S(1)} %collective-permute-done.7.refs_1_), channel_id=1, source_target_pairs={{0,1},{1,0},{2,3},{3,2},{4,5},{5,4},{6,7},{7,6},{8,9},{9,8},{10,11... | collective-permute-start | bytes 417800 | tf_op jit(solution)/shard_map/ppermute | solution.py:116
  37.8 2.8 %collective-permute-start.12 = (bf16[136,512]{1,0:T(8,128)(2,1)S(1)}, bf16[136,512]{1,0:T(8,128)(2,1)S(1)}, u32[]{:S(2)}, u32[]{:S(2)}) collective-permute-start(bf16[136,512]{1,0:T(8,128)(2,1)S(1)} %collective-permute-done.8.refs_2_), channel_id=1, source_target_pairs={{0,1},{1,0},{2,3},{3,2},{4,5},{5,4},{6,7},{7,6},{8,9},{9,8},{10,11... | collective-permute-start | bytes 417800 | tf_op jit(solution)/shard_map/ppermute | solution.py:116
  37.9 2.8 %collective-permute-start.13 = (bf16[136,512]{1,0:T(8,128)(2,1)S(1)}, bf16[136,512]{1,0:T(8,128)(2,1)S(1)}, u32[]{:S(2)}, u32[]{:S(2)}) collective-permute-start(bf16[136,512]{1,0:T(8,128)(2,1)S(1)} %collective-permute-done.9.refs_3_), channel_id=1, source_target_pairs={{0,1},{1,0},{2,3},{3,2},{4,5},{5,4},{6,7},{7,6},{8,9},{9,8},{10,11... | collective-permute-start | bytes 417800 | tf_op jit(solution)/shard_map/ppermute | solution.py:116
  38.3 2.3 %collective-permute-start.14 = (bf16[136,512]{1,0:T(8,128)(2,1)S(1)}, bf16[136,512]{1,0:T(8,128)(2,1)S(1)}, u32[]{:S(2)}, u32[]{:S(2)}) collective-permute-start(bf16[136,512]{1,0:T(8,128)(2,1)S(1)} %collective-permute-done.10.refs_4_), channel_id=1, source_target_pairs={{0,1},{1,0},{2,3},{3,2},{4,5},{5,4},{6,7},{7,6},{8,9},{9,8},{10,11... | collective-permute-start | bytes 417800 | tf_op jit(solution)/shard_map/ppermute | solution.py:116
  40.6 5.7 %copy-start.1 = (bf16[512,2048]{1,0:T(8,128)(2,1)S(1)}, bf16[512,2048]{1,0:T(8,128)(2,1)}, u32[]{:S(2)}) copy-start(bf16[512,2048]{1,0:T(8,128)(2,1)} %refs_8_.7) | copy-start | bytes 6291460
  40.6 5.7 %copy-start.2 = (bf16[2048,512]{1,0:T(8,128)(2,1)S(1)}, bf16[2048,512]{1,0:T(8,128)(2,1)}, u32[]{:S(2)}) copy-start(bf16[2048,512]{1,0:T(8,128)(2,1)} %refs_9_.9) | copy-start | bytes 6291460
  42.8 3.6 %copy-start = (bf16[512,2048]{1,0:T(8,128)(2,1)S(1)}, bf16[512,2048]{1,0:T(8,128)(2,1)}, u32[]{:S(2)}) copy-start(bf16[512,2048]{1,0:T(8,128)(2,1)} %refs_7_.7) | copy-start | bytes 6291460
  42.8 3.6 %copy-start.3 = (bf16[512,512]{1,0:T(8,128)(2,1)S(1)}, bf16[512,512]{1,0:T(8,128)(2,1)}, u32[]{:S(2)}) copy-start(bf16[512,512]{1,0:T(8,128)(2,1)} %refs_6_.7) | copy-start | bytes 1572868
  42.8 3.6 %copy-start.6 = (f32[512]{0:T(512)S(1)}, f32[512]{0:T(512)}, u32[]{:S(2)}) copy-start(f32[512]{0:T(512)} %param.24) | copy-start | bytes 6148
  45.0 1.4 %collective-permute-start.15 = (bf16[256,256]{1,0:T(8,128)(2,1)S(1)}, bf16[256,256]{1,0:T(8,128)(2,1)S(1)}, u32[]{:S(2)}, u32[]{:S(2)}) collective-permute-start(bf16[256,256]{1,0:T(8,128)(2,1)S(1)} %get-tuple-element.57), channel_id=1, source_target_pairs={{0,1},{1,0},{2,3},{3,2},{4,5},{5,4},{6,7},{7,6},{8,9},{9,8},{10,11... | collective-permute-start | bytes 393224 | tf_op jit(solution)/shard_map/ppermute | solution.py:116
  51.2 6.7 %collective-permute-start.16 = (bf16[256,256]{1,0:T(8,128)(2,1)S(1)}, bf16[256,256]{1,0:T(8,128)(2,1)S(1)}, u32[]{:S(2)}, u32[]{:S(2)}) collective-permute-start(bf16[256,256]{1,0:T(8,128)(2,1)S(1)} %get-tuple-element.62), channel_id=1, source_target_pairs={{0,1},{1,0},{2,3},{3,2},{4,5},{5,4},{6,7},{7,6},{8,9},{9,8},{10,11... | collective-permute-start | bytes 393224 | tf_op jit(solution)/shard_map/ppermute | solution.py:116
  51.4 23.5 %collective-permute-start.24 = (bf16[128,512]{1,0:T(8,128)(2,1)S(1)}, bf16[128,512]{1,0:T(8,128)(2,1)S(1)}, u32[]{:S(2)}, u32[]{:S(2)}) collective-permute-start(bf16[128,512]{1,0:T(8,128)(2,1)S(1)} %get-tuple-element.59.refs_0_), channel_id=1, source_target_pairs={{0,12},{1,13},{2,14},{3,15},{4,8},{5,9},{6,10},{7,11},{8,4},{9,5},... | collective-permute-start | bytes 393224 | tf_op jit(solution)/shard_map/ppermute | solution.py:109
  54.5 19.9 %collective-permute-start.25 = (bf16[128,512]{1,0:T(8,128)(2,1)S(1)}, bf16[128,512]{1,0:T(8,128)(2,1)S(1)}, u32[]{:S(2)}, u32[]{:S(2)}) collective-permute-start(bf16[128,512]{1,0:T(8,128)(2,1)S(1)} %get-tuple-element.72), channel_id=1, source_target_pairs={{0,14},{1,15},{2,12},{3,13},{4,10},{5,11},{6,8},{7,9},{8,6},{9,7},... | collective-permute-start | bytes 393224 | tf_op jit(solution)/shard_map/ppermute | solution.py:109
  57.1 10.1 %collective-permute-start.17 = (bf16[256,256]{1,0:T(8,128)(2,1)S(1)}, bf16[256,256]{1,0:T(8,128)(2,1)S(1)}, u32[]{:S(2)}, u32[]{:S(2)}) collective-permute-start(bf16[256,256]{1,0:T(8,128)(2,1)S(1)} %get-tuple-element.65), channel_id=1, source_target_pairs={{0,1},{1,0},{2,3},{3,2},{4,5},{5,4},{6,7},{7,6},{8,9},{9,8},{10,11... | collective-permute-start | bytes 393224 | tf_op jit(solution)/shard_map/ppermute | solution.py:116
  60.6 18.0 %collective-permute-start.22 = (bf16[128,512]{1,0:T(8,128)(2,1)S(1)}, bf16[128,512]{1,0:T(8,128)(2,1)S(1)}, u32[]{:S(2)}, u32[]{:S(2)}) collective-permute-start(bf16[128,512]{1,0:T(8,128)(2,1)S(1)} %get-tuple-element.63.refs_0_), channel_id=1, source_target_pairs={{0,8},{1,9},{2,10},{3,11},{4,12},{5,13},{6,14},{7,15},{8,0},{9,1},... | collective-permute-start | bytes 393224 | tf_op jit(solution)/shard_map/ppermute | solution.py:109
  66.8 3.7 %collective-permute-start.18 = (bf16[256,256]{1,0:T(8,128)(2,1)S(1)}, bf16[256,256]{1,0:T(8,128)(2,1)S(1)}, u32[]{:S(2)}, u32[]{:S(2)}) collective-permute-start(bf16[256,256]{1,0:T(8,128)(2,1)S(1)} %get-tuple-element.67), channel_id=1, source_target_pairs={{0,1},{1,0},{2,3},{3,2},{4,5},{5,4},{6,7},{7,6},{8,9},{9,8},{10,11... | collective-permute-start | bytes 393224 | tf_op jit(solution)/shard_map/ppermute | solution.py:116
  67.2 11.4 %collective-permute-start.23 = (bf16[128,512]{1,0:T(8,128)(2,1)S(1)}, bf16[128,512]{1,0:T(8,128)(2,1)S(1)}, u32[]{:S(2)}, u32[]{:S(2)}) collective-permute-start(bf16[128,512]{1,0:T(8,128)(2,1)S(1)} %get-tuple-element.71), channel_id=1, source_target_pairs={{0,10},{1,11},{2,8},{3,9},{4,14},{5,15},{6,12},{7,13},{8,2},{9,3},... | collective-permute-start | bytes 393224 | tf_op jit(solution)/shard_map/ppermute | solution.py:109
  70.5 12.8 %collective-permute-start.20 = (bf16[128,512]{1,0:T(8,128)(2,1)S(1)}, bf16[128,512]{1,0:T(8,128)(2,1)S(1)}, u32[]{:S(2)}, u32[]{:S(2)}) collective-permute-start(bf16[128,512]{1,0:T(8,128)(2,1)S(1)} %get-tuple-element.66.refs_0_), channel_id=1, source_target_pairs={{0,4},{1,5},{2,6},{3,7},{4,0},{5,1},{6,2},{7,3},{8,12},{9,13},{10,... | collective-permute-start | bytes 393224 | tf_op jit(solution)/shard_map/ppermute | solution.py:109
  74.4 8.9 %collective-permute-start.21 = (bf16[128,512]{1,0:T(8,128)(2,1)S(1)}, bf16[128,512]{1,0:T(8,128)(2,1)S(1)}, u32[]{:S(2)}, u32[]{:S(2)}) collective-permute-start(bf16[128,512]{1,0:T(8,128)(2,1)S(1)} %get-tuple-element.70), channel_id=1, source_target_pairs={{0,6},{1,7},{2,4},{3,5},{4,2},{5,3},{6,0},{7,1},{8,14},{9,15},{10,... | collective-permute-start | bytes 393224 | tf_op jit(solution)/shard_map/ppermute | solution.py:109
  74.9 9.0 %collective-permute-start.19 = (bf16[128,512]{1,0:T(8,128)(2,1)S(1)}, bf16[128,512]{1,0:T(8,128)(2,1)S(1)}, u32[]{:S(2)}, u32[]{:S(2)}) collective-permute-start(bf16[128,512]{1,0:T(8,128)(2,1)S(1)} %get-tuple-element.69), channel_id=1, source_target_pairs={{0,2},{1,3},{2,0},{3,1},{4,6},{5,7},{6,4},{7,5},{8,10},{9,11},{10,... | collective-permute-start | bytes 393224 | tf_op jit(solution)/shard_map/ppermute | solution.py:109
where the time goes:
time: 86.6 us; the launch traced here: 85.6 us
  Pallas kernels  32.6 us (38%)
  starting transfers between devices  28.1 us (32%)
  waiting for transfers between devices  23.3 us (27%)
  between operations  0.88 us (1%)
    ppermute x14, waiting for transfers between devices, across(): return lax.ppermute(a, self.axis, pairs)  22.1 us
    ppermute x14, starting transfers between devices, across(): return lax.ppermute(a, self.axis, pairs)  21.3 us
    pallas_call x4, Pallas kernels, dense(): pl.pallas_call(lambda *refs: body(*refs[len(after):]), grid=(1,), in_spec...  10.5 us
    pallas_call x4, Pallas kernels, spatial(): pl.pallas_call(lambda notes_ref, *refs: body(notes_ref, *refs[len(after):...  8.57 us
    pallas_call x1, Pallas kernels, temporal(): pl.pallas_call(functools.partial(temporal_kernel, plan), grid=(1,), in_sp...  7.81 us
    ppermute x12, starting transfers between devices, within(): return lax.ppermute(a, self.axis, pairs)  6.87 us
    pallas_call x2, Pallas kernels, project(): pl.pallas_call(lambda *refs: body(*refs[len(after):]), grid=(1,), in_spec...  4.05 us
  transfers between devices with their start and end apart: 26, of which 6 were waited for; matrix products, arithmetic and copies ran while one was open for 0% of the time, Pallas kernels for 16%

commit v1 on v0

--- a/solution.py
+++ b/solution.py
@@ -11,10 +11,11 @@
 HEAD_DIM = 64
 EPS = 1e-05
 NEG = -1e30
-PIECES = 4
 NOTE = 8
 AHEAD_T = 8
 AHEAD_S = 3
+AHEAD_D = 2
+CHUNK = 256
 MIB = 1 << 20
 
 
@@ -97,6 +98,11 @@
         self.cells = block // devices
         assert devices % steps == 0 and block % devices == 0
 
+    def pieces(self):
+        quarter = self.half // 2
+        runs = [(self.half, self.half + quarter), (self.half + quarter, self.steps), (0, self.half)]
+        return [tuple(range(a, b))[::-1] for a, b in runs]
+
     def place(self):
         me = lax.axis_index(self.axis)
         return me, me // self.share, me % self.share
@@ -162,24 +168,25 @@
         for peer, out_ref in enumerate(outs):
             when = slot ^ peer
             for lane in range(0, width, 128):
-                out_ref[here, lane : lane + 128] = rows_ref[
+                row = pl.multiple_of(lane // 128 * plan.block + g * part, 8)
+                out_ref[pl.ds(row, part), :] = rows_ref[
                     lane // 128, pl.ds(when, part, stride=steps), :
                 ].astype(bf16)
 
     n = plan.devices
-    lane = lax.broadcasted_iota(jnp.int32, (NOTE, width), 1)
+    lane = lax.broadcasted_iota(jnp.int32, (NOTE, 128), 1)
     note = jnp.where(lane == 0, count_ref[0], 0)
     for i in range(nbr_ref.shape[1]):
         hop = (nbr_ref[0, i] - me + n + n // 2) % n - n // 2
         note = jnp.where(lane == i + 1, hop, note)
     note = note.astype(f32).astype(bf16)
     for out_ref in outs:
-        out_ref[plan.block :, :] = note
+        out_ref[plan.block * width // 128 :, :] = note
 
 
 def temporal(plan, frames, gain, wq, wkv, wo, nbr, count):
     block, steps, width = frames.shape
-    messages = [block + NOTE] * steps
+    message = (block * width // 128 + NOTE, 128)
     smem = pl.BlockSpec(memory_space=pltpu.SMEM)
     stay = lambda a: pltpu.with_memory_space_constraint(a, pltpu.MemorySpace.HBM)
     arrays = [frames, gain.reshape(1, width), wq, wkv, wo]
@@ -187,9 +194,9 @@
         functools.partial(temporal_kernel, plan),
         grid=(1,),
         in_specs=[smem, smem] + [whole(a.shape) for a in arrays],
-        out_specs=[whole((m, width)) for m in messages],
+        out_specs=[whole(message)] * steps,
         scratch_shapes=[pltpu.VMEM((width // 128, block // 4 * steps, 128), f32)],
-        out_shape=[jax.ShapeDtypeStruct((m, width), bf16) for m in messages],
+        out_shape=[jax.ShapeDtypeStruct(message, bf16)] * steps,
         compiler_params=pltpu.CompilerParams(vmem_limit_bytes=24 * MIB),
         cost_estimate=pl.CostEstimate(
             flops=2 * block * steps * width * width * 4, bytes_accessed=6 * MIB, transcendentals=0
@@ -212,8 +219,12 @@
         spaced_ref = rest[-1]
         for (d, r), piece in zip(labels, ins):
             source = ((slot ^ r) & (half - 1)) * share + (member + share - d) % share
-            spaced_ref[:, at(source, cells), :] = piece[: spots * cells, :].astype(f32).reshape(spots, cells, width)
-            note = piece[spots * cells :, :128].astype(f32)[:1]
+            for lane in range(0, width, 128):
+                row = lane // 128 * plan.block
+                spaced_ref[:, at(source, cells), lane : lane + 128] = (
+                    piece[row : row + plan.block, :].astype(f32).reshape(spots, cells, 128)
+                )
+            note = piece[width // 128 * plan.block :, :].astype(f32)[:1]
             rest[7][pl.ds(source, 1), :] = note.astype(jnp.int32)
     step = 4
     mine = width // share
@@ -239,7 +250,7 @@
     labels = list(pieces)
     spots = plan.devices
     ins = [pieces[label] for label in labels]
-    width = ins[0].shape[1]
+    width = weights[0].shape[0]
     part = len(labels) * plan.cells
     mine = width // plan.share
     stacked = plan.cells % 8 != 0
@@ -250,9 +261,10 @@
         d = (member + plan.share - source % plan.share) % plan.share
         r = (source // plan.share) ^ (slot & (plan.half - 1))
         pile = jnp.take(jnp.stack(ins), d * plan.half + r, axis=0)
-        notes = [pile[:, spots * plan.cells, :128].astype(jnp.int32)]
-        rows = pile[:, : spots * plan.cells].reshape(len(labels), spots, plan.cells, width)
-        ins = [rows.transpose(1, 0, 2, 3).reshape(spots * part, width)]
+        tall = width // 128 * plan.block
+        notes = [pile[:, tall].astype(jnp.int32)]
+        rows = pile[:, :tall].reshape(len(labels), width // 128, spots, plan.cells, 128)
+        ins = [rows.transpose(2, 0, 3, 1, 4).reshape(spots * part, width)]
     out = [((spots * part, mine), bf16)] * 3 + [((spots * part, width), bf16)]
     if not stacked:
         out.append(((len(labels), 128), jnp.int32))
@@ -348,13 +360,17 @@
         after += mm(contexts[d][...], wo_ref[at(source, mine), :])
     after = after.astype(bf16).astype(f32)
     x = normed(after, gain_ref[...])
-    chunk = 512
     total = after
-    for start in range(0, gate_ref.shape[1], chunk):
-        gate = mm(x, gate_ref[:, start : start + chunk])
-        up = mm(x, up_ref[:, start : start + chunk])
+    starts = list(range(0, gate_ref.shape[1], CHUNK))
+    wide = lambda start: (mm(x, gate_ref[:, start : start + CHUNK]), mm(x, up_ref[:, start : start + CHUNK]))
+    ready = [wide(start) for start in starts[:AHEAD_D]]
+    for i, start in enumerate(starts):
+        if i + AHEAD_D < len(starts):
+            ready.append(wide(starts[i + AHEAD_D]))
+        gate, up = ready[i]
+        ready[i] = None
         hidden = (gate / (1.0 + jnp.exp(-gate)) * up).astype(bf16)
-        total += mm(hidden, down_ref[start : start + chunk, :])
+        total += mm(hidden, down_ref[start : start + CHUNK, :])
     for k, out_ref in enumerate(outs):
         out_ref[...] = total[k * block : (k + 1) * block].astype(bf16)
 
@@ -436,8 +452,7 @@
     early, x_early, (notes_early,) = project(plan, shared(range(half)), norm_space, weights)
     late, x_late, (notes_late,) = project(plan, shared(range(half, steps)), norm_space, weights, (x_early,))
 
-    each = steps // PIECES
-    peers = [tuple(range(i * each, (i + 1) * each)) for i in range(PIECES)][::-1]
+    peers = plan.pieces()
     mlp = (norm_mlp, s_wo, w_gate, w_up, w_down)
     landed = [None] * steps
 
@@ -457,9 +472,7 @@
     c1, last = scores(1, last)
     c2, last = scores(2, last)
     last = finish(1, c1, last)
-    c3, last = scores(3, last)
-    last = finish(2, c2, last)
-    finish(3, c3, last)
+    finish(2, c2, last)
     return gather(plan, landed)
 
 

time: 86.6 us -> 88.2 us (1.018)
  the two profiles are of different devices: /device:TPU:1 before, /device:TPU:0 now
where the time goes in v1:
time: 88.2 us; the launch traced here: 88 us
  Pallas kernels  30.1 us (34%)
  starting transfers between devices  29.7 us (34%)
  waiting for transfers between devices  26.7 us (30%)
    ppermute x14, starting transfers between devices, across(): return lax.ppermute(a, self.axis, pairs)  26.9 us
    ppermute x14, waiting for transfers between devices, across(): return lax.ppermute(a, self.axis, pairs)  25.3 us
    pallas_call x3, Pallas kernels, dense(): pl.pallas_call(lambda *refs: body(*refs[len(after):]), grid=(1,), in_spec...  8.65 us
    pallas_call x3, Pallas kernels, spatial(): pl.pallas_call(lambda notes_ref, *refs: body(notes_ref, *refs[len(after):...  7.82 us
    pallas_call x1, Pallas kernels, temporal(): pl.pallas_call(functools.partial(temporal_kernel, plan), grid=(1,), in_sp...  7.81 us
    pallas_call x2, Pallas kernels, project(): pl.pallas_call(lambda *refs: body(*refs[len(after):]), grid=(1,), in_spec...  4.18 us
    ppermute x11, starting transfers between devices, within(): return lax.ppermute(a, self.axis, pairs)  2.78 us
  transfers between devices with their start and end apart: 25, of which 7 were waited for; matrix products, arithmetic and copies ran while one was open for 0% of the time, Pallas kernels for 13%

profile of v1, /device:TPU:0, one launch (start us, length us, event | category | flops | bytes accessed | tf_op | source)
XLA Modules:
  0.0 88.0 jit_solution(4683851537828184432)
XLA Ops:
  0.7 0.6 copy-done.8
  1.3 7.8 %temporal.1 = (bf16[520,128]{1,0:T(8,128)(2,1)S(1)}, bf16[520,128]{1,0:T(8,128)(2,1)S(1)}, bf16[520,128]{1,0:T(8,128)(2,1)S(1)}, bf16[520,128]{1,0:T(8,128)(2,1)...) custom-call(s32[1,3]{1,0:T(1,128)S(1)} %copy-done.8, ...), custom_call_target="tpu_custom_call" | custom-call | flops 2147483648 | bytes 6291456 | tf_op jit(solution)/shard_map/temporal/pallas_call | solution.py:193
  9.1 3.1 %collective-permute-start = (bf16[520,128]{1,0:T(8,128)(2,1)S(1)}, bf16[520,128]{1,0:T(8,128)(2,1)S(1)}, u32[]{:S(2)}, u32[]{:S(2)}) collective-permute-start(bf16[520,128]{1,0:T(8,128)(2,1)S(1)} %get-tuple-element.38), channel_id=1, source_target_pairs={{0,2},{1,3},{2,0},{3,1},{4,6},{5,7},{6,4},{7,5},{8,10},{9,11},{10,... | collective-permute-start | bytes 399368 | tf_op jit(solution)/shard_map/ppermute | solution.py:115
  12.2 1.6 %collective-permute-start.1 = (bf16[520,128]{1,0:T(8,128)(2,1)S(1)}, bf16[520,128]{1,0:T(8,128)(2,1)S(1)}, u32[]{:S(2)}, u32[]{:S(2)}) collective-permute-start(bf16[520,128]{1,0:T(8,128)(2,1)S(1)} %get-tuple-element.39), channel_id=1, source_target_pairs={{0,4},{1,5},{2,6},{3,7},{4,0},{5,1},{6,2},{7,3},{8,12},{9,13},{10,... | collective-permute-start | bytes 399368 | tf_op jit(solution)/shard_map/ppermute | solution.py:115
  13.8 0.0 collective-permute-start.2
  13.8 3.0 %collective-permute-start.7 = (bf16[520,128]{1,0:T(8,128)(2,1)S(1)}, bf16[520,128]{1,0:T(8,128)(2,1)S(1)}, u32[]{:S(2)}, u32[]{:S(2)}) collective-permute-start(bf16[520,128]{1,0:T(8,128)(2,1)S(1)} %get-tuple-element.43), channel_id=1, source_target_pairs={{0,8},{1,9},{2,10},{3,11},{4,12},{5,13},{6,14},{7,15},{8,0},{9,1},... | collective-permute-start | bytes 399368 | tf_op jit(solution)/shard_map/ppermute | solution.py:115
  16.7 1.3 %collective-permute-start.8 = (bf16[520,128]{1,0:T(8,128)(2,1)S(1)}, bf16[520,128]{1,0:T(8,128)(2,1)S(1)}, u32[]{:S(2)}, u32[]{:S(2)}) collective-permute-start(bf16[520,128]{1,0:T(8,128)(2,1)S(1)} %get-tuple-element.44), channel_id=1, source_target_pairs={{0,10},{1,11},{2,8},{3,9},{4,14},{5,15},{6,12},{7,13},{8,2},{9,3},... | collective-permute-start | bytes 399368 | tf_op jit(solution)/shard_map/ppermute | solution.py:115
  18.1 3.6 %collective-permute-start.9 = (bf16[520,128]{1,0:T(8,128)(2,1)S(1)}, bf16[520,128]{1,0:T(8,128)(2,1)S(1)}, u32[]{:S(2)}, u32[]{:S(2)}) collective-permute-start(bf16[520,128]{1,0:T(8,128)(2,1)S(1)} %get-tuple-element.45), channel_id=1, source_target_pairs={{0,12},{1,13},{2,14},{3,15},{4,8},{5,9},{6,10},{7,11},{8,4},{9,5},... | collective-permute-start | bytes 399368 | tf_op jit(solution)/shard_map/ppermute | solution.py:115
  21.6 1.5 %collective-permute-done.1.refs_2_ = bf16[520,128]{1,0:T(8,128)(2,1)S(1)} collective-permute-done((bf16[520,128]{1,0:T(8,128)(2,1)S(1)}, bf16[520,128]{1,0:T(8,128)(2,1)S(1)}, u32[]{:S(2)}, u32[]{:S(2)}) %collective-permute-start.1) | collective-permute-done | bytes 133152 | tf_op jit(solution)/shard_map/ppermute | solution.py:115
  23.1 0.7 collective-permute-start.10
  23.8 0.0 collective-permute-done.2.refs_3_
  23.8 0.0 collective-permute-start.3
  23.8 0.0 collective-permute-done.7.refs_1_
  23.8 0.5 collective-permute-start.4
  24.3 12.2 %collective-permute-done.8.refs_2_ = bf16[520,128]{1,0:T(8,128)(2,1)S(1)} collective-permute-done((bf16[520,128]{1,0:T(8,128)(2,1)S(1)}, bf16[520,128]{1,0:T(8,128)(2,1)S(1)}, u32[]{:S(2)}, u32[]{:S(2)}) %collective-permute-start.8) | collective-permute-done | bytes 133152 | tf_op jit(solution)/shard_map/ppermute | solution.py:115
  36.5 0.5 collective-permute-start.6
  37.0 0.1 collective-permute-start.11
  37.1 0.4 collective-permute-start.12
  37.5 0.1 collective-permute-start.13
  37.6 0.2 collective-permute-done.5.refs_6_
  37.8 0.2 collective-permute-start.14
  38.1 2.0 %project.2 = (bf16[1024,256]{1,0:T(8,128)(2,1)S(1)}, bf16[1024,256]{1,0:T(8,128)(2,1)S(1)}, bf16[1024,256]{1,0:T(8,128)(2,1)S(1)}, bf16[1024,512]{1,0:T(8,128)(2,1)S(1)}, s32[8,128]{1,0:T(8,128)S(1)}) custom-call(bf16[520,128]{1,0:T(8,128)(2,1)S(1)} %get-tuple-element.37.refs_0_, bf16[520,128]{1,0:T(8,128)(2,1)S(1)} %collective-permute-done.refs_1_, ...), custom_call_target="tpu_custom_call" | custom-call | flops 805306368 | bytes 4194304 | tf_op jit(solution)/shard_map/project/pallas_call | solution.py:273
  40.1 0.0 copy-start.1
  40.1 0.0 copy-start.2
  40.1 2.2 %project.3 = (bf16[1024,256]{1,0:T(8,128)(2,1)S(1)}, bf16[1024,256]{1,0:T(8,128)(2,1)S(1)}, bf16[1024,256]{1,0:T(8,128)(2,1)S(1)}, bf16[1024,512]{1,0:T(8,128)(2,1)S(1)}, s32[8,128]{1,0:T(8,128)S(1)}) custom-call(bf16[1024,512]{1,0:T(8,128)(2,1)S(1)} %get-tuple-element.42.refs_0_.refs_3_, bf16[520,128]{1,0:T(8,128)(2,1)S(1)} %collective-permute-done.7.refs_1_, ...), custom_call_target="tpu_custom_call" | custom-call | flops 805306368 | bytes 4194304 | tf_op jit(solution)/shard_map/project/pallas_call | solution.py:273
  42.3 0.0 copy-start
  42.3 0.0 copy-start.3
  42.4 0.0 copy-start.6
  42.4 2.2 %spatial.3 = (bf16[256,256]{1,0:T(8,128)(2,1)S(1)}, bf16[256,256]{1,0:T(8,128)(2,1)S(1)}) custom-call(s32[8,128]{1,0:T(8,128)S(1)} %get-tuple-element.47.notes_ref, bf16[1024,256]{1,0:T(8,128)(2,1)S(1)} %get-tuple-element.48.refs_0_.refs_1_, bf16[1024,256]{1,0:T(8,128)(2,1)S(1)} %get-tuple-element.49.refs_1_.refs_2_, ...), custom_call_target="tpu_custom_call" | custom-call | flops 536870912 | bytes 3145728 | tf_op jit(solution)/shard_map/spatial/pallas_call | solution.py:327
  44.6 0.3 collective-permute-start.15
  44.9 1.1 %collective-permute-done.15.refs_2_ = bf16[256,256]{1,0:T(8,128)(2,1)S(1)} collective-permute-done((bf16[256,256]{1,0:T(8,128)(2,1)S(1)}, bf16[256,256]{1,0:T(8,128)(2,1)S(1)}, u32[]{:S(2)}, u32[]{:S(2)}) %collective-permute-start.15) | collective-permute-done | bytes 131104 | tf_op jit(solution)/shard_map/ppermute | solution.py:122
  46.0 2.3 %dense.3 = (bf16[128,512]{1,0:T(8,128)(2,1)S(1)}, bf16[128,512]{1,0:T(8,128)(2,1)S(1)}) custom-call(bf16[256,256]{1,0:T(8,128)(2,1)S(1)} %get-tuple-element.54.refs_0_.refs_1_, bf16[256,256]{1,0:T(8,128)(2,1)S(1)} %get-tuple-element.54.refs_0_.refs_1_, bf16[256,256]{1,0:T(8,128)(2,1)S(1)} %collective-permute-done.15.refs_2_, ...), custom_call_target="tpu_custom_call" | custom-call | flops 1744830464 | bytes 8388608 | tf_op jit(solution)/shard_map/dense/pallas_call | solution.py:384
  48.3 2.2 %spatial.4 = (bf16[256,256]{1,0:T(8,128)(2,1)S(1)}, bf16[256,256]{1,0:T(8,128)(2,1)S(1)}) custom-call(s32[8,128]{1,0:T(8,128)S(1)} %get-tuple-element.47.notes_ref, bf16[128,512]{1,0:T(8,128)(2,1)S(1)} %get-tuple-element.57.refs_0_, bf16[1024,256]{1,0:T(8,128)(2,1)S(1)} %get-tuple-element.48.refs_0_.refs_1_, ...), custom_call_target="tpu_custom_call" | custom-call | flops 536870912 | bytes 3145728 | tf_op jit(solution)/shard_map/spatial/pallas_call | solution.py:327
  50.5 0.3 collective-permute-start.16
  50.8 3.5 %spatial.5 = (bf16[512,256]{1,0:T(8,128)(2,1)S(1)}, bf16[512,256]{1,0:T(8,128)(2,1)S(1)}) custom-call(s32[8,128]{1,0:T(8,128)S(1)} %get-tuple-element.41.notes_ref, bf16[256,256]{1,0:T(8,128)(2,1)S(1)} %get-tuple-element.58.refs_0_.refs_1_, bf16[1024,256]{1,0:T(8,128)(2,1)S(1)} %get-tuple-element.48.refs_0_.refs_1_, ...), custom_call_target="tpu_custom_call" | custom-call | flops 1073741824 | bytes 3145728 | tf_op jit(solution)/shard_map/spatial/pallas_call | solution.py:327
  54.3 0.3 collective-permute-start.17
  54.6 6.1 %collective-permute-start.22 = (bf16[128,512]{1,0:T(8,128)(2,1)S(1)}, bf16[128,512]{1,0:T(8,128)(2,1)S(1)}, u32[]{:S(2)}, u32[]{:S(2)}) collective-permute-start(bf16[128,512]{1,0:T(8,128)(2,1)S(1)} %get-tuple-element.57.refs_0_), channel_id=1, source_target_pairs={{0,10},{1,11},{2,8},{3,9},{4,14},{5,15},{6,12},{7,13},{8,2},{9,3},... | collective-permute-start | bytes 393224 | tf_op jit(solution)/shard_map/ppermute | solution.py:115
  60.7 0.0 collective-permute-start.21
  60.7 2.3 %dense.4 = (bf16[128,512]{1,0:T(8,128)(2,1)S(1)}, bf16[128,512]{1,0:T(8,128)(2,1)S(1)}) custom-call(bf16[512,256]{1,0:T(8,128)(2,1)S(1)} %get-tuple-element.59.refs_0_.refs_1_, bf16[256,256]{1,0:T(8,128)(2,1)S(1)} %get-tuple-element.58.refs_0_.refs_1_, bf16[256,256]{1,0:T(8,128)(2,1)S(1)} %collective-permute-done.16.refs_2_, ...), custom_call_target="tpu_custom_call" | custom-call | flops 1744830464 | bytes 8388608 | tf_op jit(solution)/shard_map/dense/pallas_call | solution.py:384
  63.0 0.9 %collective-permute-start.23 = (bf16[128,512]{1,0:T(8,128)(2,1)S(1)}, bf16[128,512]{1,0:T(8,128)(2,1)S(1)}, u32[]{:S(2)}, u32[]{:S(2)}) collective-permute-start(bf16[128,512]{1,0:T(8,128)(2,1)S(1)} %get-tuple-element.68), channel_id=1, source_target_pairs={{0,12},{1,13},{2,14},{3,15},{4,8},{5,9},{6,10},{7,11},{8,4},{9,5},... | collective-permute-start | bytes 393224 | tf_op jit(solution)/shard_map/ppermute | solution.py:115
  63.9 3.9 %collective-permute-start.24 = (bf16[128,512]{1,0:T(8,128)(2,1)S(1)}, bf16[128,512]{1,0:T(8,128)(2,1)S(1)}, u32[]{:S(2)}, u32[]{:S(2)}) collective-permute-start(bf16[128,512]{1,0:T(8,128)(2,1)S(1)} %get-tuple-element.61.refs_0_), channel_id=1, source_target_pairs={{0,14},{1,15},{2,12},{3,13},{4,10},{5,11},{6,8},{7,9},{8,6},{9,7},... | collective-permute-start | bytes 393224 | tf_op jit(solution)/shard_map/ppermute | solution.py:115
  67.8 4.1 %dense.5 = (bf16[128,512]{1,0:T(8,128)(2,1)S(1)}, bf16[128,512]{1,0:T(8,128)(2,1)S(1)}, bf16[128,512]{1,0:T(8,128)(2,1)S(1)}, bf16[128,512]{1,0:T(8,128)(2,1)S(1)}) custom-call(bf16[128,512]{1,0:T(8,128)(2,1)S(1)} %get-tuple-element.61.refs_0_, bf16[512,256]{1,0:T(8,128)(2,1)S(1)} %get-tuple-element.59.refs_0_.refs_1_, ...), custom_call_target="tpu_custom_call" | custom-call | flops 3489660928 | bytes 8388608 | tf_op jit(solution)/shard_map/dense/pallas_call | solution.py:384
  71.9 0.6 collective-permute-start.18
  72.5 6.4 %collective-permute-done.21.refs_4_ = bf16[128,512]{1,0:T(8,128)(2,1)S(1)} collective-permute-done((bf16[128,512]{1,0:T(8,128)(2,1)S(1)}, bf16[128,512]{1,0:T(8,128)(2,1)S(1)}, u32[]{:S(2)}, u32[]{:S(2)}) %collective-permute-start.21) | collective-permute-done | bytes 131104 | tf_op jit(solution)/shard_map/ppermute | solution.py:115
  79.0 2.2 %collective-permute-start.20 = (bf16[128,512]{1,0:T(8,128)(2,1)S(1)}, bf16[128,512]{1,0:T(8,128)(2,1)S(1)}, u32[]{:S(2)}, u32[]{:S(2)}) collective-permute-start(bf16[128,512]{1,0:T(8,128)(2,1)S(1)} %get-tuple-element.66), channel_id=1, source_target_pairs={{0,6},{1,7},{2,4},{3,5},{4,2},{5,3},{6,0},{7,1},{8,14},{9,15},{10,... | collective-permute-start | bytes 393224 | tf_op jit(solution)/shard_map/ppermute | solution.py:115
  81.2 3.9 %collective-permute-done.19.refs_2_ = bf16[128,512]{1,0:T(8,128)(2,1)S(1)} collective-permute-done((bf16[128,512]{1,0:T(8,128)(2,1)S(1)}, bf16[128,512]{1,0:T(8,128)(2,1)S(1)}, u32[]{:S(2)}, u32[]{:S(2)}) %collective-permute-start.19) | collective-permute-done | bytes 131104 | tf_op jit(solution)/shard_map/ppermute | solution.py:115
  85.1 1.2 %collective-permute-done.20.refs_3_ = bf16[128,512]{1,0:T(8,128)(2,1)S(1)} collective-permute-done((bf16[128,512]{1,0:T(8,128)(2,1)S(1)}, bf16[128,512]{1,0:T(8,128)(2,1)S(1)}, u32[]{:S(2)}, u32[]{:S(2)}) %collective-permute-start.20) | collective-permute-done | bytes 131104 | tf_op jit(solution)/shard_map/ppermute | solution.py:115
  86.3 1.7 %gather.1 = bf16[128,8,512]{2,1,0:T(8,128)(2,1)} custom-call(bf16[128,512]{1,0:T(8,128)(2,1)S(1)} %get-tuple-element.63.refs_0_, bf16[128,512]{1,0:T(8,128)(2,1)S(1)} %collective-permute-done.18.refs_1_, bf16[128,512]{1,0:T(8,128)(2,1)S(1)} %collective-permute-done.19.refs_2_, bf16[128,512]{1,0:T(8,128)(2,1)S(1)} %collective-permute-done.20.refs_3_, ...), custom_call_target="tpu_custom_call" | custom-call | flops 1048576 | bytes 2097152 | tf_op jit(solution)/shard_map/gather/pallas_call | solution.py:419
  (30 shorter events, 0.1 us)
Async XLA Ops:
  0.7 0.7 copy-start.8
  1.3 36.7 %copy-start.4 = (bf16[512,1024]{1,0:T(8,128)(2,1)S(1)}, bf16[512,1024]{1,0:T(8,128)(2,1)}, u32[]{:S(2)}) copy-start(bf16[512,1024]{1,0:T(8,128)(2,1)} %refs_11_.1) | copy-start | bytes 3145732
  1.3 36.7 %copy-start.5 = (bf16[512,512]{1,0:T(8,128)(2,1)S(1)}, bf16[512,512]{1,0:T(8,128)(2,1)}, u32[]{:S(2)}) copy-start(bf16[512,512]{1,0:T(8,128)(2,1)} %refs_10_.3) | copy-start | bytes 1572868
  1.3 36.8 %copy-start.7 = (f32[512]{0:T(512)S(1)}, f32[512]{0:T(512)}, u32[]{:S(2)}) copy-start(f32[512]{0:T(512)} %param.20) | copy-start | bytes 6148
  9.1 8.9 %collective-permute-start = (bf16[520,128]{1,0:T(8,128)(2,1)S(1)}, bf16[520,128]{1,0:T(8,128)(2,1)S(1)}, u32[]{:S(2)}, u32[]{:S(2)}) collective-permute-start(bf16[520,128]{1,0:T(8,128)(2,1)S(1)} %get-tuple-element.38), channel_id=1, source_target_pairs={{0,2},{1,3},{2,0},{3,1},{4,6},{5,7},{6,4},{7,5},{8,10},{9,11},{10,... | collective-permute-start | bytes 399368 | tf_op jit(solution)/shard_map/ppermute | solution.py:115
  12.2 10.9 %collective-permute-start.1 = (bf16[520,128]{1,0:T(8,128)(2,1)S(1)}, bf16[520,128]{1,0:T(8,128)(2,1)S(1)}, u32[]{:S(2)}, u32[]{:S(2)}) collective-permute-start(bf16[520,128]{1,0:T(8,128)(2,1)S(1)} %get-tuple-element.39), channel_id=1, source_target_pairs={{0,4},{1,5},{2,6},{3,7},{4,0},{5,1},{6,2},{7,3},{8,12},{9,13},{10,... | collective-permute-start | bytes 399368 | tf_op jit(solution)/shard_map/ppermute | solution.py:115
  13.8 10.0 %collective-permute-start.2 = (bf16[520,128]{1,0:T(8,128)(2,1)S(1)}, bf16[520,128]{1,0:T(8,128)(2,1)S(1)}, u32[]{:S(2)}, u32[]{:S(2)}) collective-permute-start(bf16[520,128]{1,0:T(8,128)(2,1)S(1)} %get-tuple-element.40), channel_id=1, source_target_pairs={{0,6},{1,7},{2,4},{3,5},{4,2},{5,3},{6,0},{7,1},{8,14},{9,15},{10,... | collective-permute-start | bytes 399368 | tf_op jit(solution)/shard_map/ppermute | solution.py:115
  13.8 10.0 %collective-permute-start.7 = (bf16[520,128]{1,0:T(8,128)(2,1)S(1)}, bf16[520,128]{1,0:T(8,128)(2,1)S(1)}, u32[]{:S(2)}, u32[]{:S(2)}) collective-permute-start(bf16[520,128]{1,0:T(8,128)(2,1)S(1)} %get-tuple-element.43), channel_id=1, source_target_pairs={{0,8},{1,9},{2,10},{3,11},{4,12},{5,13},{6,14},{7,15},{8,0},{9,1},... | collective-permute-start | bytes 399368 | tf_op jit(solution)/shard_map/ppermute | solution.py:115
  16.7 19.7 %collective-permute-start.8 = (bf16[520,128]{1,0:T(8,128)(2,1)S(1)}, bf16[520,128]{1,0:T(8,128)(2,1)S(1)}, u32[]{:S(2)}, u32[]{:S(2)}) collective-permute-start(bf16[520,128]{1,0:T(8,128)(2,1)S(1)} %get-tuple-element.44), channel_id=1, source_target_pairs={{0,10},{1,11},{2,8},{3,9},{4,14},{5,15},{6,12},{7,13},{8,2},{9,3},... | collective-permute-start | bytes 399368 | tf_op jit(solution)/shard_map/ppermute | solution.py:115
  18.1 18.4 %collective-permute-start.9 = (bf16[520,128]{1,0:T(8,128)(2,1)S(1)}, bf16[520,128]{1,0:T(8,128)(2,1)S(1)}, u32[]{:S(2)}, u32[]{:S(2)}) collective-permute-start(bf16[520,128]{1,0:T(8,128)(2,1)S(1)} %get-tuple-element.45), channel_id=1, source_target_pairs={{0,12},{1,13},{2,14},{3,15},{4,8},{5,9},{6,10},{7,11},{8,4},{9,5},... | collective-permute-start | bytes 399368 | tf_op jit(solution)/shard_map/ppermute | solution.py:115
  23.1 13.9 %collective-permute-start.10 = (bf16[520,128]{1,0:T(8,128)(2,1)S(1)}, bf16[520,128]{1,0:T(8,128)(2,1)S(1)}, u32[]{:S(2)}, u32[]{:S(2)}) collective-permute-start(bf16[520,128]{1,0:T(8,128)(2,1)S(1)} %get-tuple-element.46), channel_id=1, source_target_pairs={{0,14},{1,15},{2,12},{3,13},{4,10},{5,11},{6,8},{7,9},{8,6},{9,7},... | collective-permute-start | bytes 399368 | tf_op jit(solution)/shard_map/ppermute | solution.py:115
  23.8 13.3 %collective-permute-start.3 = (bf16[520,128]{1,0:T(8,128)(2,1)S(1)}, bf16[520,128]{1,0:T(8,128)(2,1)S(1)}, u32[]{:S(2)}, u32[]{:S(2)}) collective-permute-start(bf16[520,128]{1,0:T(8,128)(2,1)S(1)} %get-tuple-element.37.refs_0_), channel_id=1, source_target_pairs={{0,1},{1,0},{2,3},{3,2},{4,5},{5,4},{6,7},{7,6},{8,9},{9,8},{10,11... | collective-permute-start | bytes 399368 | tf_op jit(solution)/shard_map/ppermute | solution.py:122
  23.8 13.7 %collective-permute-start.4 = (bf16[520,128]{1,0:T(8,128)(2,1)S(1)}, bf16[520,128]{1,0:T(8,128)(2,1)S(1)}, u32[]{:S(2)}, u32[]{:S(2)}) collective-permute-start(bf16[520,128]{1,0:T(8,128)(2,1)S(1)} %collective-permute-done.refs_1_), channel_id=1, source_target_pairs={{0,1},{1,0},{2,3},{3,2},{4,5},{5,4},{6,7},{7,6},{8,9},{9,8},{10,11... | collective-permute-start | bytes 399368 | tf_op jit(solution)/shard_map/ppermute | solution.py:122
  36.5 1.4 %collective-permute-start.5 = (bf16[520,128]{1,0:T(8,128)(2,1)S(1)}, bf16[520,128]{1,0:T(8,128)(2,1)S(1)}, u32[]{:S(2)}, u32[]{:S(2)}) collective-permute-start(bf16[520,128]{1,0:T(8,128)(2,1)S(1)} %collective-permute-done.1.refs_2_), channel_id=1, source_target_pairs={{0,1},{1,0},{2,3},{3,2},{4,5},{5,4},{6,7},{7,6},{8,9},{9,8},{10,11... | collective-permute-start | bytes 399368 | tf_op jit(solution)/shard_map/ppermute | solution.py:122
  36.5 1.5 %collective-permute-start.6 = (bf16[520,128]{1,0:T(8,128)(2,1)S(1)}, bf16[520,128]{1,0:T(8,128)(2,1)S(1)}, u32[]{:S(2)}, u32[]{:S(2)}) collective-permute-start(bf16[520,128]{1,0:T(8,128)(2,1)S(1)} %collective-permute-done.2.refs_3_), channel_id=1, source_target_pairs={{0,1},{1,0},{2,3},{3,2},{4,5},{5,4},{6,7},{7,6},{8,9},{9,8},{10,11... | collective-permute-start | bytes 399368 | tf_op jit(solution)/shard_map/ppermute | solution.py:122
  37.0 3.1 %collective-permute-start.11 = (bf16[520,128]{1,0:T(8,128)(2,1)S(1)}, bf16[520,128]{1,0:T(8,128)(2,1)S(1)}, u32[]{:S(2)}, u32[]{:S(2)}) collective-permute-start(bf16[520,128]{1,0:T(8,128)(2,1)S(1)} %collective-permute-done.7.refs_1_), channel_id=1, source_target_pairs={{0,1},{1,0},{2,3},{3,2},{4,5},{5,4},{6,7},{7,6},{8,9},{9,8},{10,11... | collective-permute-start | bytes 399368 | tf_op jit(solution)/shard_map/ppermute | solution.py:122
  37.1 3.0 %collective-permute-start.12 = (bf16[520,128]{1,0:T(8,128)(2,1)S(1)}, bf16[520,128]{1,0:T(8,128)(2,1)S(1)}, u32[]{:S(2)}, u32[]{:S(2)}) collective-permute-start(bf16[520,128]{1,0:T(8,128)(2,1)S(1)} %collective-permute-done.8.refs_2_), channel_id=1, source_target_pairs={{0,1},{1,0},{2,3},{3,2},{4,5},{5,4},{6,7},{7,6},{8,9},{9,8},{10,11... | collective-permute-start | bytes 399368 | tf_op jit(solution)/shard_map/ppermute | solution.py:122
  37.5 2.6 %collective-permute-start.13 = (bf16[520,128]{1,0:T(8,128)(2,1)S(1)}, bf16[520,128]{1,0:T(8,128)(2,1)S(1)}, u32[]{:S(2)}, u32[]{:S(2)}) collective-permute-start(bf16[520,128]{1,0:T(8,128)(2,1)S(1)} %collective-permute-done.9.refs_3_), channel_id=1, source_target_pairs={{0,1},{1,0},{2,3},{3,2},{4,5},{5,4},{6,7},{7,6},{8,9},{9,8},{10,11... | collective-permute-start | bytes 399368 | tf_op jit(solution)/shard_map/ppermute | solution.py:122
  37.8 2.3 %collective-permute-start.14 = (bf16[520,128]{1,0:T(8,128)(2,1)S(1)}, bf16[520,128]{1,0:T(8,128)(2,1)S(1)}, u32[]{:S(2)}, u32[]{:S(2)}) collective-permute-start(bf16[520,128]{1,0:T(8,128)(2,1)S(1)} %collective-permute-done.10.refs_4_), channel_id=1, source_target_pairs={{0,1},{1,0},{2,3},{3,2},{4,5},{5,4},{6,7},{7,6},{8,9},{9,8},{10,11... | collective-permute-start | bytes 399368 | tf_op jit(solution)/shard_map/ppermute | solution.py:122
  40.1 5.9 %copy-start.1 = (bf16[512,2048]{1,0:T(8,128)(2,1)S(1)}, bf16[512,2048]{1,0:T(8,128)(2,1)}, u32[]{:S(2)}) copy-start(bf16[512,2048]{1,0:T(8,128)(2,1)} %refs_8_.5) | copy-start | bytes 6291460
  40.1 5.8 %copy-start.2 = (bf16[2048,512]{1,0:T(8,128)(2,1)S(1)}, bf16[2048,512]{1,0:T(8,128)(2,1)}, u32[]{:S(2)}) copy-start(bf16[2048,512]{1,0:T(8,128)(2,1)} %refs_9_.7) | copy-start | bytes 6291460
  42.3 3.6 %copy-start = (bf16[512,2048]{1,0:T(8,128)(2,1)S(1)}, bf16[512,2048]{1,0:T(8,128)(2,1)}, u32[]{:S(2)}) copy-start(bf16[512,2048]{1,0:T(8,128)(2,1)} %refs_7_.5) | copy-start | bytes 6291460
  42.3 3.6 %copy-start.3 = (bf16[512,512]{1,0:T(8,128)(2,1)S(1)}, bf16[512,512]{1,0:T(8,128)(2,1)}, u32[]{:S(2)}) copy-start(bf16[512,512]{1,0:T(8,128)(2,1)} %refs_6_.5) | copy-start | bytes 1572868
  42.4 3.6 %copy-start.6 = (f32[512]{0:T(512)S(1)}, f32[512]{0:T(512)}, u32[]{:S(2)}) copy-start(f32[512]{0:T(512)} %param.24) | copy-start | bytes 6148
  44.6 1.4 %collective-permute-start.15 = (bf16[256,256]{1,0:T(8,128)(2,1)S(1)}, bf16[256,256]{1,0:T(8,128)(2,1)S(1)}, u32[]{:S(2)}, u32[]{:S(2)}) collective-permute-start(bf16[256,256]{1,0:T(8,128)(2,1)S(1)} %get-tuple-element.55), channel_id=1, source_target_pairs={{0,1},{1,0},{2,3},{3,2},{4,5},{5,4},{6,7},{7,6},{8,9},{9,8},{10,11... | collective-permute-start | bytes 393224 | tf_op jit(solution)/shard_map/ppermute | solution.py:122
  50.5 10.2 %collective-permute-start.16 = (bf16[256,256]{1,0:T(8,128)(2,1)S(1)}, bf16[256,256]{1,0:T(8,128)(2,1)S(1)}, u32[]{:S(2)}, u32[]{:S(2)}) collective-permute-start(bf16[256,256]{1,0:T(8,128)(2,1)S(1)} %get-tuple-element.60), channel_id=1, source_target_pairs={{0,1},{1,0},{2,3},{3,2},{4,5},{5,4},{6,7},{7,6},{8,9},{9,8},{10,11... | collective-permute-start | bytes 393224 | tf_op jit(solution)/shard_map/ppermute | solution.py:122
  54.3 13.5 %collective-permute-start.17 = (bf16[512,256]{1,0:T(8,128)(2,1)S(1)}, bf16[512,256]{1,0:T(8,128)(2,1)S(1)}, u32[]{:S(2)}, u32[]{:S(2)}) collective-permute-start(bf16[512,256]{1,0:T(8,128)(2,1)S(1)} %get-tuple-element.62), channel_id=1, source_target_pairs={{0,1},{1,0},{2,3},{3,2},{4,5},{5,4},{6,7},{7,6},{8,9},{9,8},{10,11... | collective-permute-start | bytes 786440 | tf_op jit(solution)/shard_map/ppermute | solution.py:122
  54.6 24.4 %collective-permute-start.22 = (bf16[128,512]{1,0:T(8,128)(2,1)S(1)}, bf16[128,512]{1,0:T(8,128)(2,1)S(1)}, u32[]{:S(2)}, u32[]{:S(2)}) collective-permute-start(bf16[128,512]{1,0:T(8,128)(2,1)S(1)} %get-tuple-element.57.refs_0_), channel_id=1, source_target_pairs={{0,10},{1,11},{2,8},{3,9},{4,14},{5,15},{6,12},{7,13},{8,2},{9,3},... | collective-permute-start | bytes 393224 | tf_op jit(solution)/shard_map/ppermute | solution.py:115
  60.7 18.2 %collective-permute-start.21 = (bf16[128,512]{1,0:T(8,128)(2,1)S(1)}, bf16[128,512]{1,0:T(8,128)(2,1)S(1)}, u32[]{:S(2)}, u32[]{:S(2)}) collective-permute-start(bf16[128,512]{1,0:T(8,128)(2,1)S(1)} %get-tuple-element.67), channel_id=1, source_target_pairs={{0,8},{1,9},{2,10},{3,11},{4,12},{5,13},{6,14},{7,15},{8,0},{9,1},... | collective-permute-start | bytes 393224 | tf_op jit(solution)/shard_map/ppermute | solution.py:115
  63.0 18.1 %collective-permute-start.23 = (bf16[128,512]{1,0:T(8,128)(2,1)S(1)}, bf16[128,512]{1,0:T(8,128)(2,1)S(1)}, u32[]{:S(2)}, u32[]{:S(2)}) collective-permute-start(bf16[128,512]{1,0:T(8,128)(2,1)S(1)} %get-tuple-element.68), channel_id=1, source_target_pairs={{0,12},{1,13},{2,14},{3,15},{4,8},{5,9},{6,10},{7,11},{8,4},{9,5},... | collective-permute-start | bytes 393224 | tf_op jit(solution)/shard_map/ppermute | solution.py:115
  63.9 17.2 %collective-permute-start.24 = (bf16[128,512]{1,0:T(8,128)(2,1)S(1)}, bf16[128,512]{1,0:T(8,128)(2,1)S(1)}, u32[]{:S(2)}, u32[]{:S(2)}) collective-permute-start(bf16[128,512]{1,0:T(8,128)(2,1)S(1)} %get-tuple-element.61.refs_0_), channel_id=1, source_target_pairs={{0,14},{1,15},{2,12},{3,13},{4,10},{5,11},{6,8},{7,9},{8,6},{9,7},... | collective-permute-start | bytes 393224 | tf_op jit(solution)/shard_map/ppermute | solution.py:115
  71.9 9.3 %collective-permute-start.18 = (bf16[128,512]{1,0:T(8,128)(2,1)S(1)}, bf16[128,512]{1,0:T(8,128)(2,1)S(1)}, u32[]{:S(2)}, u32[]{:S(2)}) collective-permute-start(bf16[128,512]{1,0:T(8,128)(2,1)S(1)} %get-tuple-element.64), channel_id=1, source_target_pairs={{0,2},{1,3},{2,0},{3,1},{4,6},{5,7},{6,4},{7,5},{8,10},{9,11},{10,... | collective-permute-start | bytes 393224 | tf_op jit(solution)/shard_map/ppermute | solution.py:115
  79.0 6.1 %collective-permute-start.19 = (bf16[128,512]{1,0:T(8,128)(2,1)S(1)}, bf16[128,512]{1,0:T(8,128)(2,1)S(1)}, u32[]{:S(2)}, u32[]{:S(2)}) collective-permute-start(bf16[128,512]{1,0:T(8,128)(2,1)S(1)} %get-tuple-element.65), channel_id=1, source_target_pairs={{0,4},{1,5},{2,6},{3,7},{4,0},{5,1},{6,2},{7,3},{8,12},{9,13},{10,... | collective-permute-start | bytes 393224 | tf_op jit(solution)/shard_map/ppermute | solution.py:115
  79.0 7.4 %collective-permute-start.20 = (bf16[128,512]{1,0:T(8,128)(2,1)S(1)}, bf16[128,512]{1,0:T(8,128)(2,1)S(1)}, u32[]{:S(2)}, u32[]{:S(2)}) collective-permute-start(bf16[128,512]{1,0:T(8,128)(2,1)S(1)} %get-tuple-element.66), channel_id=1, source_target_pairs={{0,6},{1,7},{2,4},{3,5},{4,2},{5,3},{6,0},{7,1},{8,14},{9,15},{10,... | collective-permute-start | bytes 393224 | tf_op jit(solution)/shard_map/ppermute | solution.py:115
